TPU v7x, 32 devices: a whole 2x2x4 slice. The times are simulated.
32 devices in a mesh: group: 4 (over z), expert: 8 (over y, x, core).
Axes of the slice: x: 2, y: 2, z: 4, core: 2. Of those that a mesh axis runs over, the one named last changes fastest.
Arguments:
- group_logits: float32 [4096, 4], P(('group', 'expert')), may hold values from -6 to 6
- expert_logits: float32 [4096, 32], P(('group', 'expert')), may hold values from -6 to 6
- expert_ids: int32 [4096, 2], P(('group', 'expert')), may hold values from 0 to 31, all different within a row; in each aligned block of 128 rows (0 to 127, 128 to 255, ...) at most 16 rows name the same one
- cotangent: bfloat16 [4096, 3584], P(('group', 'expert')), may hold values from -6 to 6
- hidden_saved: bfloat16 [32, 512, 1024], P(('group', 'expert')), may hold values from -0.1875 to 0.1875
- w_down: bfloat16 [32, 1024, 3584], P(('group', 'expert')), may hold values from -0.1875 to 0.1875
Outputs:
- hidden_grad: bfloat16 [32, 512, 1024], P(('group', 'expert'))
- d_group_logits: float32 [4096, 4], P(('group', 'expert'))
- d_expert_logits: float32 [4096, 32], P(('group', 'expert'))
Inputs may be any that keep to these rules, and one draw needn't show every extreme that they name: `expert_ids`: within the 128 tokens of one device no expert is named by more than 16 choices, a bound that some block reaches; the 2 experts of a token differ.
All inputs are finite; a program needn't handle non-finite values.
Results may differ from a plain program's by a relative error of at most 0.0045.
Values may be sent and summed in bfloat16 or wider, within the bound.
No kernel may reach another device: no remote copies, remote signals or barrier semaphores. Data moves between devices by JAX's collectives and lax.ppermute only.
A program may use at most 64 MiB of HBM per device.

v0:
```python
from functools import partial

import jax
import jax.numpy as jnp
from jax import lax
from jax.sharding import PartitionSpec as P

ITERS = 5


SOFTCAP = 4.0


def capped(logits):
    return jnp.exp(SOFTCAP * jnp.tanh(logits / SOFTCAP))


def squashing(logits):
    bounded = jnp.tanh(logits / SOFTCAP)
    return 1.0 - bounded * bounded


def balance_level(level_in, target, column_sum):
    scaled = level_in * (target / column_sum)
    return (scaled, jnp.sum(scaled, -1, keepdims=True))


def adjoint_local(out_grad, level_in, target, column_sum):
    scaled, row_total = balance_level(level_in, target, column_sum)
    level_out = scaled / row_total
    scaled_grad = (out_grad - jnp.sum(out_grad * level_out, -1, keepdims=True)) / row_total
    return (scaled_grad, jnp.sum(scaled_grad * level_in, 0))


def adjoint_finish(scaled_grad, inner, target, column_sum):
    return target / column_sum * (scaled_grad - inner / column_sum)


def balance_step(targets, current, unused):
    target_group, target_expert = targets
    group_in, expert_in = current
    group_cols, expert_cols = lax.psum(
        (jnp.sum(group_in, 0), jnp.sum(expert_in, 0)), ("group", "expert")
    )
    scaled_g, rowsum_g = balance_level(group_in, target_group, group_cols)
    scaled_e, rowsum_e = balance_level(expert_in, target_expert, expert_cols)
    return (
        (scaled_g / rowsum_g, scaled_e / rowsum_e),
        (group_in, expert_in, group_cols, expert_cols),
    )


def adjoint_step(targets, carried, stored_step):
    target_group, target_expert = targets
    grad_g, grad_e = carried
    group_in, expert_in, group_cols, expert_cols = stored_step
    scaled_g, inner_g = adjoint_local(grad_g, group_in, target_group, group_cols)
    scaled_e, inner_e = adjoint_local(grad_e, expert_in, target_expert, expert_cols)
    inner_g, inner_e = lax.psum((inner_g, inner_e), ("group", "expert"))
    next_g = adjoint_finish(scaled_g, inner_g, target_group, group_cols)
    next_e = adjoint_finish(scaled_e, inner_e, target_expert, expert_cols)
    return ((next_g, next_e), None)


def deliver(payload):
    halfway = (
        lax.all_to_all(payload[0], "expert", split_axis=1, concat_axis=1, tiled=True),
        lax.all_to_all(payload[1], "expert", split_axis=1, concat_axis=1, tiled=True),
    )
    return (
        lax.all_to_all(halfway[0], "group", split_axis=0, concat_axis=0, tiled=True),
        lax.all_to_all(halfway[1], "group", split_axis=0, concat_axis=0, tiled=True),
    )


def per_device(group_logits, expert_logits, expert_ids, cotangent, hidden_saved, w_down):
    groups = lax.axis_size("group")
    per_group = lax.axis_size("expert")
    experts = groups * per_group
    tokens_here = cotangent.shape[0]
    top_count = expert_ids.shape[1]
    model_width = cotangent.shape[1]
    capacity = hidden_saved.shape[1] // experts
    targets = (float(tokens_here * per_group), float(tokens_here * groups))
    flat_ids = expert_ids.reshape(-1)
    picked = (flat_ids[:, None] == jnp.arange(experts, dtype=jnp.int32)[None, :]).astype(jnp.int32)
    positions = jnp.sum((jnp.cumsum(picked, 0) - picked) * picked, 1)
    slot_index = flat_ids * capacity + positions
    serial = jnp.arange(flat_ids.shape[0], dtype=jnp.int32)
    source_index = jnp.zeros((experts * capacity,), jnp.int32).at[slot_index].set(serial)
    filled = jnp.zeros((experts * capacity,), jnp.int32).at[slot_index].set(1)
    fetched = jnp.take(cotangent, source_index // top_count, axis=0)
    send_rows = jnp.where(filled[:, None] > 0, fetched, jnp.zeros_like(fetched))
    send_rows = send_rows.reshape(groups, per_group, capacity, model_width)
    group_of = expert_ids // per_group
    group_aff = capped(group_logits)
    expert_aff = capped(expert_logits).reshape(tokens_here, groups, per_group)
    (group_prob, expert_prob), stored = lax.scan(
        partial(balance_step, targets), (group_aff, expert_aff), None, length=ITERS
    )
    pick_group = jnp.take_along_axis(group_prob, group_of, 1)
    pick_expert = jnp.take_along_axis(expert_prob.reshape(tokens_here, experts), expert_ids, 1)
    pair_prob = pick_group * pick_expert
    total_prob = jnp.sum(pair_prob, 1, keepdims=True)
    gate_prob = pair_prob / total_prob
    gate_sent = (
        jnp.zeros((experts * capacity,), jnp.bfloat16)
        .at[slot_index]
        .set(gate_prob.astype(jnp.bfloat16).reshape(-1))
    )
    gate_sent = gate_sent.reshape(groups, per_group, capacity)
    routed = (
        group_aff,
        expert_aff,
        stored,
        pick_group,
        pick_expert,
        total_prob,
        gate_prob,
        gate_sent,
    )
    got_rows, got_gates = deliver((send_rows, routed[7]))
    group_aff, expert_aff, stored, pick_group, pick_expert, total_prob, gate_prob, unused_gates = (
        routed
    )
    weight = w_down[0]
    saved_hidden = hidden_saved[0]
    expert_rows = got_rows.reshape(-1, model_width)
    unscaled = lax.dot_general(
        expert_rows, weight, (((1,), (1,)), ((), ())), preferred_element_type=jnp.float32
    )
    slot_grad = jnp.sum(unscaled * saved_hidden.astype(jnp.float32), 1)
    grad_rows = (got_gates.reshape(-1, 1).astype(jnp.float32) * unscaled).astype(jnp.bfloat16)
    hidden_grad = grad_rows[None]
    answers = lax.all_to_all(
        lax.all_to_all(
            slot_grad.reshape(groups, per_group, capacity),
            "group",
            split_axis=0,
            concat_axis=0,
            tiled=True,
        ),
        "expert",
        split_axis=1,
        concat_axis=1,
        tiled=True,
    )
    gate_grad = answers.reshape(-1)[slot_index].reshape(tokens_here, top_count)
    pair_grad = (gate_grad - jnp.sum(gate_prob * gate_grad, 1, keepdims=True)) / total_prob
    group_pick = (
        group_of[:, :, None] == jnp.arange(groups, dtype=jnp.int32)[None, None, :]
    ).astype(jnp.float32)
    seed_group = jnp.sum(group_pick * (pair_grad * pick_expert)[:, :, None], 1)
    expert_pick = (
        expert_ids[:, :, None] == jnp.arange(experts, dtype=jnp.int32)[None, None, :]
    ).astype(jnp.float32)
    seed_expert = jnp.sum(expert_pick * (pair_grad * pick_group)[:, :, None], 1).reshape(
        tokens_here, groups, per_group
    )
    (grad_group, grad_expert), unused = lax.scan(
        partial(adjoint_step, targets), (seed_group, seed_expert), stored, reverse=True
    )
    d_group_logits = grad_group * group_aff * squashing(group_logits)
    d_expert_logits = (grad_expert * expert_aff).reshape(tokens_here, experts) * squashing(
        expert_logits
    )
    return (hidden_grad, d_group_logits, d_expert_logits)


def solution(mesh):
    in_specs = (
        P(("group", "expert"), None),
        P(("group", "expert"), None),
        P(("group", "expert"), None),
        P(("group", "expert"), None),
        P(("group", "expert"), None, None),
        P(("group", "expert"), None, None),
    )
    out_specs = (
        P(("group", "expert"), None, None),
        P(("group", "expert"), None),
        P(("group", "expert"), None),
    )
    return jax.shard_map(
        per_device, mesh=mesh, in_specs=in_specs, out_specs=out_specs, check_vma=False
    )
```

profile of v0, /device:TPU:0, one launch (start us, length us, event | category | flops | bytes accessed | tf_op | source)
XLA Modules:
  0.0 600.4 jit_solution(14312915412681843163)
XLA Ops:
  0.6 0.9 copy.101
  1.5 0.1 eq.55
  1.7 0.1 eq.51
  1.8 0.7 broadcast_multiply_fusion
  2.5 0.6 reduce-window.6
  3.1 0.2 slice_reduce_fusion
  3.4 0.1 mul.222
  3.7 1.4 scatter_custom_fusion.2
  5.2 1.4 scatter_custom_fusion.1
  6.8 4.2 gather_fusion
  10.9 3.6 fusion.16
  14.6 5.3 all-to-all-start.2
  20.1 0.1 reshape.221
  20.3 43.2 %all-to-all-done.2 = bf16[4,8,16,3584]{3,2,0,1:T(8,128)(2,1)} async-done(((bf16[4,8,16,3584]{3,2,0,1:T(8,128)(2,1)}), bf16[4,8,16,3584]{3,2,0,1:T(8,128)(2,1)}, u32[]{:S(2)}, u32[]{:S(2)}) %all-to-all-start.2) | async-done | bytes 3670048 | tf_op jit(solution)/shard_map/all_to_all | solution.py:67
  63.5 4.2 copy.114
  67.6 5.6 all-to-all-start.3
  73.2 264.1 %while.36 = (s32[]{:T(128)}, f32[128,4]{0,1:T(4,128)S(1)}, f32[128,4,8]{0,2,1:T(8,128)S(1)}, f32[5,128,4]{1,2,0:T(4,128)S(1)}, f32[5,128,4,8]{1,3,2,0:T(8,128)S(...) while((s32[]{:T(128)}, f32[128,4]{0,1:T(4,128)S(1)}, ...), condition=%wide.region_10.11_spmd, body=%wide.region_3.10_spmd.sunk | while | flops 15277 | bytes 133133 | solution.py:98
  73.4 100.2 %all-reduce.4 = (f32[4]{0:T(128)S(1)}, f32[4,8]{1,0:T(4,128)S(1)}) all-reduce(f32[4]{0:T(128)S(1)} %reduce_sum.212, f32[4,8]{1,0:T(4,128)S(1)} %reduce_sum.213), channel_id=1, replica_groups=mesh['group'=4,'expert'=8] {'group','expert'}, use_global_device_ids=true, to_apply=%region_5.5 | all-reduce | flops 36 | bytes 288 | tf_op jit(solution)/shard_map/while/body/eval_jaxpr/psum | solution.py:42
  173.9 0.3 fusion.45
  174.4 39.5 %all-reduce.4 = (f32[4]{0:T(128)S(1)}, f32[4,8]{1,0:T(4,128)S(1)}) all-reduce(f32[4]{0:T(128)S(1)} %reduce_sum.212, f32[4,8]{1,0:T(4,128)S(1)} %reduce_sum.213), channel_id=1, replica_groups=mesh['group'=4,'expert'=8] {'group','expert'}, use_global_device_ids=true, to_apply=%region_5.5 | all-reduce | flops 36 | bytes 288 | tf_op jit(solution)/shard_map/while/body/eval_jaxpr/psum | solution.py:42
  214.2 0.3 fusion.45
  214.7 40.5 %all-reduce.4 = (f32[4]{0:T(128)S(1)}, f32[4,8]{1,0:T(4,128)S(1)}) all-reduce(f32[4]{0:T(128)S(1)} %reduce_sum.212, f32[4,8]{1,0:T(4,128)S(1)} %reduce_sum.213), channel_id=1, replica_groups=mesh['group'=4,'expert'=8] {'group','expert'}, use_global_device_ids=true, to_apply=%region_5.5 | all-reduce | flops 36 | bytes 288 | tf_op jit(solution)/shard_map/while/body/eval_jaxpr/psum | solution.py:42
  255.4 0.3 fusion.45
  256.0 39.4 %all-reduce.4 = (f32[4]{0:T(128)S(1)}, f32[4,8]{1,0:T(4,128)S(1)}) all-reduce(f32[4]{0:T(128)S(1)} %reduce_sum.212, f32[4,8]{1,0:T(4,128)S(1)} %reduce_sum.213), channel_id=1, replica_groups=mesh['group'=4,'expert'=8] {'group','expert'}, use_global_device_ids=true, to_apply=%region_5.5 | all-reduce | flops 36 | bytes 288 | tf_op jit(solution)/shard_map/while/body/eval_jaxpr/psum | solution.py:42
  295.6 0.3 fusion.45
  296.1 40.6 %all-reduce.4 = (f32[4]{0:T(128)S(1)}, f32[4,8]{1,0:T(4,128)S(1)}) all-reduce(f32[4]{0:T(128)S(1)} %reduce_sum.212, f32[4,8]{1,0:T(4,128)S(1)} %reduce_sum.213), channel_id=1, replica_groups=mesh['group'=4,'expert'=8] {'group','expert'}, use_global_device_ids=true, to_apply=%region_5.5 | all-reduce | flops 36 | bytes 288 | tf_op jit(solution)/shard_map/while/body/eval_jaxpr/psum | solution.py:42
  336.9 0.3 fusion.45
  337.3 2.4 gather_fusion.2
  339.7 0.1 reshape.224
  340.0 0.1 reshape.227
  340.1 2.0 gather_fusion.3
  342.3 8.4 %fusion.17 = (f32[512]{0:T(512)S(1)}, f32[512,1024]{1,0:T(8,128)S(1)}) fusion(bf16[1,512,1024]{2,1,0:T(8,128)(2,1)} %param.14, bf16[512,3584]{1,0:T(8,128)(2,1)} %bitcast.18, bf16[1,1024,3584]{2,1,0:T(8,128)(2,1)} %param.15), kind=kOutput, calls=%fused_computation.49 | convolution fusion | flops 3759668736 | bytes 14157824 | tf_op jit(solution)/shard_map/dot_general | solution.py:129
  350.8 0.7 reshape.275
  351.5 3.4 all-to-all-start.4
  354.9 5.5 all-to-all-done.4
  360.4 0.5 broadcast.296
  360.9 0.7 reduce.2
  361.6 0.6 copy.115
  362.2 4.6 all-to-all-start.5
  366.9 4.7 all-to-all-done.5
  371.7 1.9 gather_fusion.1
  373.9 204.3 %while.37 = (s32[]{:T(128)}, f32[128,4]{0,1:T(4,128)S(1)}, f32[128,4,8]{0,2,1:T(8,128)S(1)}, f32[5,4]{1,0:T(8,128)S(1)}, f32[5,128,4]{1,2,0:T(4,128)S(1)}, /*ind...) while((s32[]{:T(128)}, f32[128,4]{0,1:T(4,128)S(1)}, ...), condition=%wide.region_28.29_spmd, body=%wide.region_19.28_spmd.sunk | while | flops 52050 | bytes 159945 | solution.py:160
  374.1 0.6 fusion.50
  375.0 38.3 %all-reduce.5 = (f32[4]{0:T(128)S(1)}, f32[4,8]{1,0:T(4,128)S(1)}) all-reduce(f32[4]{0:T(128)S(1)} %fusion.48, f32[4,8]{1,0:T(4,128)S(1)} %get-tuple-element.338), channel_id=1, replica_groups=mesh['group'=4,'expert'=8] {'group','expert'}, use_global_device_ids=true, to_apply=%region_23.23 | all-reduce | flops 36 | bytes 288 | tf_op jit(solution)/shard_map/while/body/eval_jaxpr/psum | solution.py:59
  413.5 0.6 fusion.50
  414.5 40.1 %all-reduce.5 = (f32[4]{0:T(128)S(1)}, f32[4,8]{1,0:T(4,128)S(1)}) all-reduce(f32[4]{0:T(128)S(1)} %fusion.48, f32[4,8]{1,0:T(4,128)S(1)} %get-tuple-element.338), channel_id=1, replica_groups=mesh['group'=4,'expert'=8] {'group','expert'}, use_global_device_ids=true, to_apply=%region_23.23 | all-reduce | flops 36 | bytes 288 | tf_op jit(solution)/shard_map/while/body/eval_jaxpr/psum | solution.py:59
  454.9 0.6 fusion.50
  455.8 39.9 %all-reduce.5 = (f32[4]{0:T(128)S(1)}, f32[4,8]{1,0:T(4,128)S(1)}) all-reduce(f32[4]{0:T(128)S(1)} %fusion.48, f32[4,8]{1,0:T(4,128)S(1)} %get-tuple-element.338), channel_id=1, replica_groups=mesh['group'=4,'expert'=8] {'group','expert'}, use_global_device_ids=true, to_apply=%region_23.23 | all-reduce | flops 36 | bytes 288 | tf_op jit(solution)/shard_map/while/body/eval_jaxpr/psum | solution.py:59
  496.0 0.6 fusion.50
  496.9 40.1 %all-reduce.5 = (f32[4]{0:T(128)S(1)}, f32[4,8]{1,0:T(4,128)S(1)}) all-reduce(f32[4]{0:T(128)S(1)} %fusion.48, f32[4,8]{1,0:T(4,128)S(1)} %get-tuple-element.338), channel_id=1, replica_groups=mesh['group'=4,'expert'=8] {'group','expert'}, use_global_device_ids=true, to_apply=%region_23.23 | all-reduce | flops 36 | bytes 288 | tf_op jit(solution)/shard_map/while/body/eval_jaxpr/psum | solution.py:59
  537.3 0.6 fusion.50
  538.3 39.8 %all-reduce.5 = (f32[4]{0:T(128)S(1)}, f32[4,8]{1,0:T(4,128)S(1)}) all-reduce(f32[4]{0:T(128)S(1)} %fusion.48, f32[4,8]{1,0:T(4,128)S(1)} %get-tuple-element.338), channel_id=1, replica_groups=mesh['group'=4,'expert'=8] {'group','expert'}, use_global_device_ids=true, to_apply=%region_23.23 | all-reduce | flops 36 | bytes 288 | tf_op jit(solution)/shard_map/while/body/eval_jaxpr/psum | solution.py:59
  578.3 0.1 copy.108
  578.4 0.2 reshape.237
  578.6 2.2 scatter_custom_fusion
  580.8 0.6 copy.109
  581.5 3.6 all-to-all-start
  585.0 0.6 bitcast_multiply_fusion.4
  585.6 4.1 all-to-all-done
  589.7 0.6 copy.110
  590.3 3.2 all-to-all-start.1
  593.6 0.6 subtract_multiply_fusion.2
  594.2 5.0 all-to-all-done.1
  599.2 1.2 fusion.18
  (156 shorter events, 6.7 us)
Async XLA Ops:
  0.6 6.1 %copy-start = (bf16[128,3584]{1,0:T(8,128)(2,1)S(1)}, bf16[128,3584]{1,0:T(8,128)(2,1)}, u32[]{:S(2)}) copy-start(bf16[128,3584]{1,0:T(8,128)(2,1)} %param.13) | copy-start | bytes 2752516
  14.6 5.4 copy-start.2
  14.6 5.7 copy-start.3
  14.6 5.7 copy-start.1
  14.6 48.9 %all-to-all-start.2 = ((bf16[4,8,16,3584]{3,2,0,1:T(8,128)(2,1)}), bf16[4,8,16,3584]{3,2,0,1:T(8,128)(2,1)}, u32[]{:S(2)}, u32[]{:S(2)}) async-start(bf16[4,8,16,3584]{3,2,0,1:T(8,128)(2,1)} %fusion.16), calls=%async_computation.2 | async-start | bytes 7340032 | tf_op jit(solution)/shard_map/all_to_all | solution.py:67
  67.6 274.7 %all-to-all-start.3 = ((bf16[4,8,16,3584]{3,2,1,0:T(8,128)(2,1)}), bf16[4,8,16,3584]{3,2,1,0:T(8,128)(2,1)}, u32[]{:S(2)}, u32[]{:S(2)}) async-start(bf16[4,8,16,3584]{3,2,1,0:T(8,128)(2,1)} %copy.114), calls=%async_computation.3 | async-start | bytes 7340032 | tf_op jit(solution)/shard_map/all_to_all | solution.py:71
  351.5 8.9 %all-to-all-start.4 = ((f32[4,1,128]{2,1,0:T(1,128)}), f32[4,1,128]{2,1,0:T(1,128)S(1)}, u32[]{:S(2)}, u32[]{:S(2)}) async-start(f32[4,1,128]{2,1,0:T(1,128)} %reshape.275), calls=%async_computation.4 | async-start | bytes 4096 | tf_op jit(solution)/shard_map/all_to_all | solution.py:136
  362.2 9.4 %all-to-all-start.5 = ((f32[4,8,16]{2,0,1:T(4,128)}), f32[4,8,16]{2,0,1:T(4,128)S(1)}, u32[]{:S(2)}, u32[]{:S(2)}) async-start(f32[4,8,16]{2,0,1:T(4,128)} %copy.115), calls=%async_computation.5 | async-start | bytes 32768 | tf_op jit(solution)/shard_map/all_to_all | solution.py:135
  581.5 8.3 %all-to-all-start = ((bf16[4,8,16]{2,0,1:T(4,128)(2,1)}), bf16[4,8,16]{2,0,1:T(4,128)(2,1)S(1)}, u32[]{:S(2)}, u32[]{:S(2)}) async-start(bf16[4,8,16]{2,0,1:T(4,128)(2,1)} %copy.109), calls=%async_computation | async-start | bytes 16384 | tf_op jit(solution)/shard_map/all_to_all | solution.py:68
  590.3 8.8 %all-to-all-start.1 = ((bf16[4,8,16]{2,1,0:T(8,128)(2,1)}), bf16[4,8,16]{2,1,0:T(8,128)(2,1)S(1)}, u32[]{:S(2)}, u32[]{:S(2)}) async-start(bf16[4,8,16]{2,1,0:T(8,128)(2,1)} %copy.110), calls=%async_computation.1 | async-start | bytes 16384 | tf_op jit(solution)/shard_map/all_to_all | solution.py:72
where the time goes:
time: 602 us; the launch traced here: 600 us
  blocking collectives  458 us (76%)
  waiting for transfers between devices  62.5 us (10%)
  local copies, waits for them, and re-layouts  26.5 us (4%)
  starting transfers between devices  25.7 us (4%)
  other arithmetic  17.9 us (3%)
  matrix products  8.44 us (1%)
    psum x5, blocking collectives, balance_step(): lax.psum((jnp.sum(group_in, 0), jnp.sum(expert_in, 0)), ('group', 'expert'))  260 us
    psum x5, blocking collectives, adjoint_step(): inner_g, inner_e = lax.psum((inner_g, inner_e), ('group', 'expert'))  198 us
    all_to_all x1, waiting for transfers between devices, deliver(): lax.all_to_all(payload[0], 'expert', split_axis=1, concat_axis=1, tiled=T...  43.2 us
  transfers between devices with their start and end apart: 6, of which 5 were waited for; matrix products, arithmetic and copies ran while one was open for 2% of the time, Pallas kernels for 0%

commit v1 on v0

v1 whole, which is shorter than its diff:
```python
from functools import partial

import jax
import jax.numpy as jnp
from jax import lax
from jax.experimental import pallas as pl
from jax.experimental.pallas import tpu as pltpu
from jax.sharding import PartitionSpec as P

ITERS = 5
SOFTCAP = 4.0
LANES = 128
SUBLANES = 8
AXES = ("group", "expert")
REPLICATED_BYTES = 1 << 20


def capped(logits):
    return jnp.exp(SOFTCAP * jnp.tanh(logits / SOFTCAP))


def squashing(logits):
    bounded = jnp.tanh(logits / SOFTCAP)
    return 1.0 - bounded * bounded


def balance_level(level_in, target, column_sum):
    scaled = level_in * (target / column_sum)
    return (scaled, jnp.sum(scaled, -1, keepdims=True))


def adjoint_local(out_grad, level_in, target, column_sum):
    scaled, row_total = balance_level(level_in, target, column_sum)
    level_out = scaled / row_total
    scaled_grad = (out_grad - jnp.sum(out_grad * level_out, -1, keepdims=True)) / row_total
    return (scaled_grad, jnp.sum(scaled_grad * level_in, 0))


def adjoint_finish(scaled_grad, inner, target, column_sum):
    return target / column_sum * (scaled_grad - inner / column_sum)


def balance_step(targets, current, unused):
    target_group, target_expert = targets
    group_in, expert_in = current
    group_cols, expert_cols = lax.psum((jnp.sum(group_in, 0), jnp.sum(expert_in, 0)), AXES)
    scaled_g, rowsum_g = balance_level(group_in, target_group, group_cols)
    scaled_e, rowsum_e = balance_level(expert_in, target_expert, expert_cols)
    return (
        (scaled_g / rowsum_g, scaled_e / rowsum_e),
        (group_in, expert_in, group_cols, expert_cols),
    )


def adjoint_step(targets, carried, stored_step):
    target_group, target_expert = targets
    grad_g, grad_e = carried
    group_in, expert_in, group_cols, expert_cols = stored_step
    scaled_g, inner_g = adjoint_local(grad_g, group_in, target_group, group_cols)
    scaled_e, inner_e = adjoint_local(grad_e, expert_in, target_expert, expert_cols)
    inner_g, inner_e = lax.psum((inner_g, inner_e), AXES)
    next_g = adjoint_finish(scaled_g, inner_g, target_group, group_cols)
    next_e = adjoint_finish(scaled_e, inner_e, target_expert, expert_cols)
    return ((next_g, next_e), None)


def slots_of(expert_ids, experts, capacity):
    flat_ids = expert_ids.reshape(-1)
    picked = (flat_ids[:, None] == jnp.arange(experts, dtype=jnp.int32)[None, :]).astype(jnp.int32)
    positions = jnp.sum((jnp.cumsum(picked, 0) - picked) * picked, 1)
    return flat_ids * capacity + positions


def distributed(group_logits, expert_logits, expert_ids, cotangent, hidden_saved, w_down):
    groups = lax.axis_size("group")
    per_group = lax.axis_size("expert")
    experts = groups * per_group
    tokens_here, top_count = expert_ids.shape
    model_width = cotangent.shape[1]
    capacity = hidden_saved.shape[1] // experts
    slots = experts * capacity
    targets = (float(tokens_here * per_group), float(tokens_here * groups))
    slot_index = slots_of(expert_ids, experts, capacity)
    serial = jnp.arange(slot_index.shape[0], dtype=jnp.int32)
    source_index = jnp.zeros((slots,), jnp.int32).at[slot_index].set(serial)
    filled = jnp.zeros((slots,), jnp.int32).at[slot_index].set(1)
    fetched = jnp.take(cotangent, source_index // top_count, axis=0)
    send_rows = jnp.where(filled[:, None] > 0, fetched, jnp.zeros_like(fetched))
    expert_rows = lax.all_to_all(send_rows, AXES, split_axis=0, concat_axis=0, tiled=True)
    group_of = expert_ids // per_group
    group_aff = capped(group_logits)
    expert_aff = capped(expert_logits).reshape(tokens_here, groups, per_group)
    (group_prob, expert_prob), stored = lax.scan(
        partial(balance_step, targets), (group_aff, expert_aff), None, length=ITERS
    )
    pick_group = jnp.take_along_axis(group_prob, group_of, 1)
    pick_expert = jnp.take_along_axis(expert_prob.reshape(tokens_here, experts), expert_ids, 1)
    pair_prob = pick_group * pick_expert
    total_prob = jnp.sum(pair_prob, 1, keepdims=True)
    gate_prob = pair_prob / total_prob
    gate_sent = (
        jnp.zeros((slots,), jnp.bfloat16)
        .at[slot_index]
        .set(gate_prob.astype(jnp.bfloat16).reshape(-1))
    )
    got_gates = lax.all_to_all(gate_sent, AXES, split_axis=0, concat_axis=0, tiled=True)
    unscaled = lax.dot_general(
        expert_rows, w_down[0], (((1,), (1,)), ((), ())), preferred_element_type=jnp.float32
    )
    slot_grad = jnp.sum(unscaled * hidden_saved[0].astype(jnp.float32), 1)
    grad_rows = (got_gates.reshape(-1, 1).astype(jnp.float32) * unscaled).astype(jnp.bfloat16)
    answers = lax.all_to_all(slot_grad, AXES, split_axis=0, concat_axis=0, tiled=True)
    gate_grad = answers[slot_index].reshape(tokens_here, top_count)
    pair_grad = (gate_grad - jnp.sum(gate_prob * gate_grad, 1, keepdims=True)) / total_prob
    group_pick = (
        group_of[:, :, None] == jnp.arange(groups, dtype=jnp.int32)[None, None, :]
    ).astype(jnp.float32)
    seed_group = jnp.sum(group_pick * (pair_grad * pick_expert)[:, :, None], 1)
    expert_pick = (
        expert_ids[:, :, None] == jnp.arange(experts, dtype=jnp.int32)[None, None, :]
    ).astype(jnp.float32)
    seed_expert = jnp.sum(expert_pick * (pair_grad * pick_group)[:, :, None], 1).reshape(
        tokens_here, groups, per_group
    )
    (grad_group, grad_expert), unused = lax.scan(
        partial(adjoint_step, targets), (seed_group, seed_expert), stored, reverse=True
    )
    d_group_logits = grad_group * group_aff * squashing(group_logits)
    d_expert_logits = (grad_expert * expert_aff).reshape(tokens_here, experts) * squashing(
        expert_logits
    )
    return (grad_rows[None], d_group_logits, d_expert_logits)


def pack_kernel(ids_ref, rows_ref, out_ref, place_ref, *, experts, capacity):
    tokens, top_count = ids_ref.shape
    slots = experts * capacity

    @pl.when(pl.program_id(0) == 0)
    def _():
        ids = ids_ref[...]
        columns = lax.broadcasted_iota(jnp.int32, (tokens, LANES), 1)
        chosen = [ids[:, k : k + 1] == columns for k in range(top_count)]
        picked = sum(c.astype(jnp.float32) for c in chosen)
        row = lax.broadcasted_iota(jnp.int32, (tokens, tokens), 0)
        column = lax.broadcasted_iota(jnp.int32, (tokens, tokens), 1)
        earlier = (column < row).astype(jnp.bfloat16)
        before = jnp.dot(
            earlier, picked.astype(jnp.bfloat16), preferred_element_type=jnp.float32
        )
        slot_at = lax.broadcasted_iota(jnp.int32, (tokens, slots), 1)
        place = jnp.zeros((tokens, slots), jnp.float32)
        for k in range(top_count):
            position = jnp.sum(jnp.where(chosen[k], before, 0.0), 1, keepdims=True)
            slot = ids[:, k : k + 1] * capacity + position.astype(jnp.int32)
            place = place + (slot == slot_at).astype(jnp.float32)
        place_ref[...] = place.astype(jnp.bfloat16)

    out_ref[...] = lax.dot_general(
        place_ref[...],
        rows_ref[...],
        (((0,), (0,)), ((), ())),
        preferred_element_type=jnp.float32,
    ).astype(out_ref.dtype)


def pack_rows(expert_ids, cotangent, experts, capacity):
    tokens, width = cotangent.shape
    slots = experts * capacity
    block = 512 if width % 512 == 0 else width
    return pl.pallas_call(
        partial(pack_kernel, experts=experts, capacity=capacity),
        out_shape=jax.ShapeDtypeStruct((slots, width), cotangent.dtype),
        grid=(width // block,),
        in_specs=[
            pl.BlockSpec(expert_ids.shape, lambda i: (0, 0)),
            pl.BlockSpec((tokens, block), lambda i: (0, i)),
        ],
        out_specs=pl.BlockSpec((slots, block), lambda i: (0, i)),
        scratch_shapes=[pltpu.VMEM((tokens, slots), jnp.bfloat16)],
        cost_estimate=pl.CostEstimate(
            flops=2 * tokens * slots * width,
            bytes_accessed=2 * width * (tokens + slots),
            transcendentals=0,
        ),
        name="pack_rows",
    )(expert_ids, cotangent)


def tile_rows(g):
    return pl.ds(SUBLANES * (g + 1), SUBLANES)


def forward_kernel(
    me_ref, all_ref, level_ref, inverse_ref, column_ref, seed_q_ref, seed_p_ref, where_ref,
    gate_ref, own_ref, dense_ref, before_ref, *, groups, top_count, capacity, targets
):
    devices = all_ref.shape[0]
    tiles = groups + 1
    tile = (SUBLANES, LANES)
    row_id = lax.broadcasted_iota(jnp.int32, tile, 0)
    zero = jnp.zeros(tile, jnp.float32)

    def totals(sums):
        out = []
        for i in range(tiles):
            column = jnp.sum(sums[i], 1, keepdims=True) + zero
            out.append(jnp.where(row_id < groups, column, 1.0) if i == 0 else column)
        return out

    def start(d, sums):
        new = []
        for i in range(tiles):
            rows = pl.ds(SUBLANES * i, SUBLANES)
            level = capped(all_ref[d, rows, :])
            if i == 0:
                level = jnp.where(row_id < groups, level, 0.0)
            level_ref[0, d, rows, :] = level
            new.append(sums[i] + level)
        named = [all_ref[d, groups + k : groups + k + 1, :].astype(jnp.int32) for k in range(top_count)]
        for g in range(groups):
            expert = row_id + g * SUBLANES
            hit = named[0] == expert
            for k in range(1, top_count):
                hit = hit | (named[k] == expert)
            dense_ref[d, pl.ds(SUBLANES * g, SUBLANES), :] = hit.astype(jnp.float32)
        return tuple(new)

    sums = lax.fori_loop(0, devices, start, (zero,) * tiles, unroll=2)

    for k in range(ITERS):
        columns = totals(sums)
        factors = []
        for i in range(tiles):
            column_ref[k, pl.ds(SUBLANES * i, SUBLANES), :] = columns[i]
            factors.append(targets[min(i, 1)] / columns[i])

        def step(d, sums, k=k, factors=factors):
            new = []
            for i in range(tiles):
                rows = pl.ds(SUBLANES * i, SUBLANES)
                scaled = level_ref[k, d, rows, :] * factors[i]
                inverse = 1.0 / jnp.sum(scaled, 0, keepdims=True)
                inverse_ref[k, d, pl.ds(i, 1), :] = inverse
                level = scaled * inverse
                level_ref[k + 1, d, rows, :] = level
                new.append(sums[i] + level)
            return tuple(new)

        sums = lax.fori_loop(0, devices, step, (zero,) * tiles, unroll=4)

    experts = groups * SUBLANES
    earlier = (
        lax.broadcasted_iota(jnp.int32, (LANES, LANES), 0)
        < lax.broadcasted_iota(jnp.int32, (LANES, LANES), 1)
    ).astype(jnp.bfloat16)
    before_ref[...] = jnp.dot(
        dense_ref[...].reshape(devices * experts, LANES).astype(jnp.bfloat16),
        earlier,
        preferred_element_type=jnp.float32,
    ).reshape(devices, experts, LANES)

    per_block = LANES // capacity
    slot_id = lax.broadcasted_iota(jnp.int32, (capacity, LANES), 0)
    me = me_ref[0]

    def finish(d, unused):
        picks = []
        total = jnp.zeros((1, LANES), jnp.float32)
        for g in range(groups):
            hit = dense_ref[d, pl.ds(SUBLANES * g, SUBLANES), :]
            pick_p = hit * level_ref[ITERS, d, g : g + 1, :]
            pick_q = hit * level_ref[ITERS, d, tile_rows(g), :]
            pair = pick_p * pick_q
            total = total + jnp.sum(pair, 0, keepdims=True)
            picks.append((pick_p, pick_q, pair))
        hit_me = dense_ref[d, pl.ds(me, 1), :]
        before_me = before_ref[d, pl.ds(me, 1), :].astype(jnp.int32)
        for g in range(groups):
            rows = pl.ds(SUBLANES * g, SUBLANES)
            pick_p, pick_q, pair = picks[g]
            seed_q_ref[d, rows, :] = pick_p / total
            seed_p_ref[d, rows, :] = pick_q / total
            dense_ref[d, rows, :] = pair / total
            position = before_ref[d, rows, :].astype(jnp.int32)
            lane = lax.rem(d, per_block) * capacity + position
            where_ref[d, rows, :] = jnp.minimum(lane, LANES - 1)
        gate_me = dense_ref[d, pl.ds(me, 1), :].astype(jnp.bfloat16).astype(jnp.float32)
        taken = jnp.where((before_me == slot_id) & (hit_me > 0.0), gate_me, 0.0)
        gate_ref[pl.ds(d * capacity, capacity), :] = jnp.sum(taken, 1, keepdims=True) + jnp.zeros(
            (capacity, LANES), jnp.float32
        )
        return unused

    lax.fori_loop(0, devices, finish, 0)
    for i in range(tiles):
        rows = pl.ds(SUBLANES * i, SUBLANES)
        own_ref[rows, :] = level_ref[0, me, rows, :] * squashing(all_ref[me, rows, :])


def forward(me, everyone, groups, top_count, capacity, targets):
    devices, rows, lanes = everyone.shape
    experts = groups * SUBLANES
    f32 = jnp.float32
    shapes = [
        ((ITERS + 1, devices, rows, lanes), f32),
        ((ITERS, devices, SUBLANES, lanes), f32),
        ((ITERS, rows, lanes), f32),
        ((devices, experts, lanes), f32),
        ((devices, experts, lanes), f32),
        ((devices, experts, lanes), jnp.int32),
        ((devices * capacity, lanes), f32),
        ((rows, lanes), f32),
    ]
    vmem = pl.BlockSpec(memory_space=pltpu.VMEM)
    return pl.pallas_call(
        partial(
            forward_kernel, groups=groups, top_count=top_count, capacity=capacity, targets=targets
        ),
        out_shape=[jax.ShapeDtypeStruct(s, d) for s, d in shapes],
        in_specs=[pl.BlockSpec(memory_space=pltpu.SMEM), vmem],
        out_specs=[vmem] * len(shapes),
        scratch_shapes=[
            pltpu.VMEM((devices, experts, lanes), f32),
            pltpu.VMEM((devices, experts, lanes), f32),
        ],
        cost_estimate=pl.CostEstimate(flops=10_000_000, bytes_accessed=8_000_000, transcendentals=0),
        name="forward",
    )(me, everyone)


def product_kernel(rows_ref, weight_ref, saved_ref, gate_ref, grad_ref, slot_ref, sum_ref):
    unscaled = lax.dot_general(
        rows_ref[...],
        weight_ref[...],
        (((1,), (1,)), ((), ())),
        preferred_element_type=jnp.float32,
    )
    grad_ref[...] = (gate_ref[:, :1] * unscaled).astype(grad_ref.dtype)
    partial_sums = unscaled * saved_ref[...].astype(jnp.float32)
    folded = partial_sums[:, :LANES]
    for j in range(1, partial_sums.shape[1] // LANES):
        folded = folded + partial_sums[:, j * LANES : (j + 1) * LANES]
    first = pl.program_id(0) == 0

    @pl.when(first)
    def _():
        sum_ref[...] = folded

    @pl.when(jnp.logical_not(first))
    def _():
        sum_ref[...] = sum_ref[...] + folded

    @pl.when(pl.program_id(0) == pl.num_programs(0) - 1)
    def _():
        for j in range(slot_ref.shape[1] // LANES):
            turned = sum_ref[j * LANES : (j + 1) * LANES, :].T
            slot_ref[:, j * LANES : (j + 1) * LANES] = jnp.sum(turned, 0, keepdims=True)


def product(rows, weight, saved, gates):
    slots, width = rows.shape
    hidden = weight.shape[0]
    block = 256 if hidden % 256 == 0 else hidden
    return pl.pallas_call(
        product_kernel,
        out_shape=[
            jax.ShapeDtypeStruct((slots, hidden), jnp.bfloat16),
            jax.ShapeDtypeStruct((1, slots), jnp.float32),
        ],
        grid=(hidden // block,),
        in_specs=[
            pl.BlockSpec((slots, width), lambda i: (0, 0)),
            pl.BlockSpec((block, width), lambda i: (i, 0)),
            pl.BlockSpec((slots, block), lambda i: (0, i)),
            pl.BlockSpec((slots, LANES), lambda i: (0, 0)),
        ],
        out_specs=[
            pl.BlockSpec((slots, block), lambda i: (0, i)),
            pl.BlockSpec((1, slots), lambda i: (0, 0)),
        ],
        scratch_shapes=[pltpu.VMEM((slots, LANES), jnp.float32)],
        cost_estimate=pl.CostEstimate(
            flops=2 * slots * width * hidden,
            bytes_accessed=2 * (slots * width + hidden * width + 2 * slots * hidden),
            transcendentals=0,
        ),
        name="product",
    )(rows, weight, saved, gates)


def adjoint_kernel(
    me_ref, slot_ref, level_ref, inverse_ref, column_ref, seed_q_ref, seed_p_ref, where_ref,
    own_ref, group_ref, expert_ref, carry_ref, *, groups, capacity, targets
):
    devices = level_ref.shape[1]
    tiles = groups + 1
    tile = (SUBLANES, LANES)
    row_id = lax.broadcasted_iota(jnp.int32, tile, 0)
    zero = jnp.zeros(tile, jnp.float32)
    per_block = LANES // capacity

    def seeds(d):
        block = pl.ds(pl.multiple_of(lax.div(d, per_block) * LANES, LANES), LANES)
        grads = []
        mixed = jnp.zeros((1, LANES), jnp.float32)
        for g in range(groups):
            rows = pl.ds(SUBLANES * g, SUBLANES)
            grad = jnp.take_along_axis(slot_ref[rows, block], where_ref[d, rows, :], axis=1)
            gate = seed_q_ref[d, rows, :] * level_ref[ITERS, d, tile_rows(g), :]
            mixed = mixed + jnp.sum(gate * grad, 0, keepdims=True)
            grads.append(grad)
        out = [zero]
        for g in range(groups):
            rows = pl.ds(SUBLANES * g, SUBLANES)
            grad = grads[g] - mixed
            out.append(seed_q_ref[d, rows, :] * grad)
            level = jnp.sum(seed_p_ref[d, rows, :] * grad, 0, keepdims=True)
            out[0] = jnp.where(row_id == g, level, out[0])
        return out

    def factors_of(k):
        out = []
        for i in range(tiles):
            column = column_ref[k, pl.ds(SUBLANES * i, SUBLANES), :]
            factor = targets[min(i, 1)] / column
            if i == 0:
                factor = jnp.where(row_id < groups, factor, 0.0)
            out.append((factor, column))
        return out

    inner = None
    for k in reversed(range(ITERS)):
        if inner is not None:
            scale = []
            for i, (factor, column) in enumerate(factors_of(k + 1)):
                total = jnp.sum(inner[i], 1, keepdims=True) + zero
                scale.append((factor, total / column))

        def step(d, sums, k=k):
            if k == ITERS - 1:
                grads = seeds(d)
            else:
                grads = [
                    scale[i][0] * (carry_ref[d, pl.ds(SUBLANES * i, SUBLANES), :] - scale[i][1])
                    for i in range(tiles)
                ]
            new = []
            for i in range(tiles):
                rows = pl.ds(SUBLANES * i, SUBLANES)
                along = jnp.sum(grads[i] * level_ref[k + 1, d, rows, :], 0, keepdims=True)
                scaled = (grads[i] - along) * inverse_ref[k, d, pl.ds(i, 1), :]
                carry_ref[d, rows, :] = scaled
                new.append(sums[i] + scaled * level_ref[k, d, rows, :])
            return tuple(new)

        inner = lax.fori_loop(0, devices, step, (zero,) * tiles, unroll=4)

    me = me_ref[0]
    for i, (factor, column) in enumerate(factors_of(0)):
        rows = pl.ds(SUBLANES * i, SUBLANES)
        total = jnp.sum(inner[i], 1, keepdims=True) + zero
        carry_ref[0, rows, :] = (
            factor * (carry_ref[me, rows, :] - total / column) * own_ref[rows, :]
        )
    turned = carry_ref[0, :, :].T
    group_ref[...] = turned[:, :groups]
    expert_ref[...] = turned[:, SUBLANES:]


def adjoint(me, slot_grads, saved, own, groups, capacity, targets):
    level = saved[0]
    rows, lanes = level.shape[2:]
    vmem = pl.BlockSpec(memory_space=pltpu.VMEM)
    return pl.pallas_call(
        partial(adjoint_kernel, groups=groups, capacity=capacity, targets=targets),
        out_shape=[
            jax.ShapeDtypeStruct((lanes, groups), jnp.float32),
            jax.ShapeDtypeStruct((lanes, groups * SUBLANES), jnp.float32),
        ],
        in_specs=[pl.BlockSpec(memory_space=pltpu.SMEM)] + [vmem] * (2 + len(saved)),
        out_specs=[vmem, vmem],
        scratch_shapes=[pltpu.VMEM(level.shape[1:], jnp.float32)],
        cost_estimate=pl.CostEstimate(flops=10_000_000, bytes_accessed=8_000_000, transcendentals=0),
        name="adjoint",
    )(me, slot_grads, *saved, own)


def spread(block):
    copies = jnp.broadcast_to(block[None], (lax.axis_size(AXES),) + block.shape)
    return lax.all_to_all(copies, AXES, split_axis=0, concat_axis=0)


def replicated(group_logits, expert_logits, expert_ids, cotangent, hidden_saved, w_down):
    groups = lax.axis_size("group")
    per_group = lax.axis_size("expert")
    experts = groups * per_group
    tokens_here, top_count = expert_ids.shape
    capacity = hidden_saved.shape[1] // experts
    targets = (float(tokens_here * per_group), float(tokens_here * groups))
    me = (lax.axis_index("group") * per_group + lax.axis_index("expert")).reshape(1)
    spare = SUBLANES - groups - top_count
    mine = jnp.concatenate(
        [
            group_logits,
            expert_ids.astype(jnp.float32),
            jnp.zeros((tokens_here, spare), jnp.float32),
            expert_logits,
        ],
        1,
    ).T
    everyone = spread(mine)
    send_rows = pack_rows(expert_ids, cotangent, experts, capacity)
    expert_rows = lax.all_to_all(send_rows, AXES, split_axis=0, concat_axis=0, tiled=True)
    *saved, gates, own = forward(me, everyone, groups, top_count, capacity, targets)
    hidden_grad, slot_grad = product(expert_rows, w_down[0], hidden_saved[0], gates)
    slot_grads = spread(slot_grad).reshape(experts, -1)
    d_group, d_expert = adjoint(me, slot_grads, saved, own, groups, capacity, targets)
    return (hidden_grad[None], d_group, d_expert)


def per_device(group_logits, expert_logits, expert_ids, cotangent, hidden_saved, w_down):
    groups = lax.axis_size("group")
    per_group = lax.axis_size("expert")
    tokens_here, top_count = expert_ids.shape
    capacity = hidden_saved.shape[1] // (groups * per_group)
    everyone_bytes = 4 * tokens_here * (groups * per_group) * (groups * per_group + SUBLANES)
    fits = (
        tokens_here == LANES
        and per_group == SUBLANES
        and groups + top_count <= SUBLANES
        and LANES % capacity == 0
        and capacity % SUBLANES == 0
        and everyone_bytes <= REPLICATED_BYTES
    )
    form = replicated if fits else distributed
    return form(group_logits, expert_logits, expert_ids, cotangent, hidden_saved, w_down)


def solution(mesh):
    rows = P(AXES, None)
    blocks = P(AXES, None, None)
    return jax.shard_map(
        per_device,
        mesh=mesh,
        in_specs=(rows, rows, rows, rows, blocks, blocks),
        out_specs=(blocks, rows, rows),
        check_vma=False,
    )
```

time: 602 us -> 146 us (0.24)
  blocking collectives: 458 us -> 11.3 us
  Pallas kernels: 0 us -> 31.7 us
  waiting for transfers between devices: 62.5 us -> 82.7 us
  local copies, waits for them, and re-layouts: 26.5 us -> 6.71 us
  other arithmetic: 17.9 us -> 1.48 us
  starting transfers between devices: 25.7 us -> 10.9 us
  matrix products: 8.44 us -> 0 us
    psum x10 -> x0, blocking collectives: 458 us -> none  [the longest x5 260 us: balance_step(): lax.psum((jnp.sum(group_in, 0), jnp.sum(expert_in, 0)), ('group', 'expert'))]
    pallas_call x0 -> x4, Pallas kernels: none -> 31.7 us  [the longest x1 9.69 us: forward(): pl.pallas_call(partial(forward_kernel, groups=groups, top_count=top_count...]
    all_to_all x6 -> x2, waiting for transfers between devices: 62.5 us -> 82.7 us  [the longest x1 72.8 us: replicated(): lax.all_to_all(send_rows, AXES, split_axis=0, concat_axis=0, tiled=True)]
    all_to_all x6 -> x2, starting transfers between devices: 25.7 us -> 10.9 us  [the longest x1 7.33 us: spread(): return lax.all_to_all(copies, AXES, split_axis=0, concat_axis=0)]
    gather x12 -> x0, local copies, waits for them, and re-layouts: 11.4 us -> none  [the longest x1 4.16 us: per_device(): fetched = jnp.take(cotangent, source_index // top_count, axis=0)]
    all_to_all x0 -> x1, blocking collectives: none -> 11.3 us  [spread(): return lax.all_to_all(copies, AXES, split_axis=0, concat_axis=0)]
    dot_general x1 -> x0, matrix products: 8.44 us -> none  [per_device(): lax.dot_general(expert_rows, weight, (((1,), (1,)), ((), ())), preferred_...]
  transfers between devices with their start and end apart: 6 -> 2, of which waited for: 5 -> 2; matrix products, arithmetic and copies ran while one was open for 2% -> 1% of each run, Pallas kernels for 0% -> 11%
where the time goes in v1:
time: 146 us; the launch traced here: 145 us
  waiting for transfers between devices  82.7 us (57%)
  Pallas kernels  31.7 us (22%)
  blocking collectives  11.3 us (8%)
  starting transfers between devices  10.9 us (7%)
  local copies, waits for them, and re-layouts  6.71 us (5%)
  other arithmetic  1.48 us (1%)
    all_to_all x1, waiting for transfers between devices, replicated(): lax.all_to_all(send_rows, AXES, split_axis=0, concat_axis=0, tiled=True)  72.8 us
    all_to_all x1, blocking collectives, spread(): return lax.all_to_all(copies, AXES, split_axis=0, concat_axis=0)  11.3 us
    all_to_all x1, waiting for transfers between devices, spread(): return lax.all_to_all(copies, AXES, split_axis=0, concat_axis=0)  9.93 us
    pallas_call x1, Pallas kernels, forward(): pl.pallas_call(partial(forward_kernel, groups=groups, top_count=top_count...  9.69 us
    pallas_call x1, Pallas kernels, product(): pl.pallas_call(product_kernel, out_shape=[jax.ShapeDtypeStruct((slots, hi...  8.8 us
    all_to_all x1, starting transfers between devices, spread(): return lax.all_to_all(copies, AXES, split_axis=0, concat_axis=0)  7.33 us
    pallas_call x1, Pallas kernels, pack_rows(): pl.pallas_call(partial(pack_kernel, experts=experts, capacity=capacity),...  6.65 us
    pallas_call x1, Pallas kernels, adjoint(): pl.pallas_call(partial(adjoint_kernel, groups=groups, capacity=capacity,...  6.57 us
  transfers between devices with their start and end apart: 2, of which 2 were waited for; matrix products, arithmetic and copies ran while one was open for 1% of the time, Pallas kernels for 11%

profile of v1, /device:TPU:0, one launch (start us, length us, event | category | flops | bytes accessed | tf_op | source)
XLA Modules:
  0.0 145.4 jit_solution(16665322142123838210)
XLA Ops:
  0.6 0.7 convert_element_type.3
  1.3 0.1 pad.2.clone
  1.4 0.8 maximum_bitcast_fusion
  2.2 0.9 broadcast_in_dim.21
  3.1 7.3 %all-to-all-start.1 = ((f32[32,40,128]{2,1,0:T(8,128)}), f32[32,40,128]{2,1,0:T(8,128)S(1)}, u32[]{:S(2)}, u32[]{:S(2)}) async-start(f32[32,40,128]{2,1,0:T(8,128)} %broadcast_in_dim.21), calls=%async_computation.1 | async-start | bytes 1310720 | tf_op jit(solution)/shard_map/all_to_all | solution.py:491
  10.4 1.4 copy.12.ids_ref
  11.8 6.7 %pack_rows.1 = bf16[512,3584]{1,0:T(8,128)(2,1)} custom-call(s32[128,2]{1,0:T(8,128)} %copy.12.ids_ref, bf16[128,3584]{1,0:T(8,128)(2,1)} %rows_ref.1), custom_call_target="tpu_custom_call" | custom-call | flops 469762048 | bytes 4587520 | tf_op jit(solution)/shard_map/pack_rows/pallas_call | solution.py:171
  18.5 9.9 %all-to-all-done.1.all_ref = f32[32,40,128]{2,1,0:T(8,128)S(1)} async-done(((f32[32,40,128]{2,1,0:T(8,128)}), f32[32,40,128]{2,1,0:T(8,128)S(1)}, u32[]{:S(2)}, u32[]{:S(2)}) %all-to-all-start.1) | async-done | bytes 655392 | tf_op jit(solution)/shard_map/all_to_all | solution.py:491
  28.4 0.0 copy-start
  28.4 3.5 %all-to-all-start = ((bf16[32,16,3584]{2,1,0:T(8,128)(2,1)}), bf16[32,16,3584]{2,1,0:T(8,128)(2,1)}, u32[]{:S(2)}, u32[]{:S(2)}) async-start(bf16[32,16,3584]{2,1,0:T(8,128)(2,1)} %bitcast.12), calls=%async_computation | async-start | bytes 7340032 | tf_op jit(solution)/shard_map/all_to_all | solution.py:514
  31.9 0.0 copy-done
  32.0 9.7 %forward.1 = (f32[6,32,40,128]{3,2,1,0:T(8,128)}, f32[5,32,8,128]{3,2,1,0:T(8,128)}, f32[5,40,128]{2,1,0:T(8,128)}, f32[32,32,128]{2,1,0:T(8,128)}, f32[32,32,12...) custom-call(s32[1]{0:T(128)} %bitcast.4.me_ref, f32[32,40,128]{2,1,0:T(8,128)} %copy-done), custom_call_target="tpu_custom_call" | custom-call | flops 10000000 | bytes 8000000 | tf_op jit(solution)/shard_map/forward/pallas_call | solution.py:316
  41.7 72.8 %all-to-all-done = bf16[32,16,3584]{2,1,0:T(8,128)(2,1)} async-done(((bf16[32,16,3584]{2,1,0:T(8,128)(2,1)}), bf16[32,16,3584]{2,1,0:T(8,128)(2,1)}, u32[]{:S(2)}, u32[]{:S(2)}) %all-to-all-start) | async-done | bytes 3670048 | tf_op jit(solution)/shard_map/all_to_all | solution.py:514
  114.5 8.8 %product.1 = (bf16[512,1024]{1,0:T(8,128)(2,1)}, f32[1,512]{1,0:T(1,128)}) custom-call(bf16[512,3584]{1,0:T(8,128)(2,1)} %bitcast.1.rows_ref, bf16[1024,3584]{1,0:T(8,128)(2,1)} %bitcast.15, bf16[512,1024]{1,0:T(8,128)(2,1)} %bitcast.16, f32[512,128]{1,0:T(8,128)} %get-tuple-element.15.gate_ref), custom_call_target="tpu_custom_call" | custom-call | flops 3758096384 | bytes 13107200 | tf_op jit(solution)/shard_map/product/pallas_call | solution.py:365
  123.3 0.7 broadcast_in_dim.24
  124.0 11.3 %all_to_all.21 = f32[32,1,512]{2,1,0:T(1,128)S(1)} all-to-all(f32[32,1,512]{2,1,0:T(1,128)S(1)} %broadcast_in_dim.24), channel_id=1, replica_groups=mesh['group'=4,'expert'=8] {'group','expert'}, dimensions={0} | all-to-all | bytes 131072 | tf_op jit(solution)/shard_map/all_to_all | solution.py:491
  135.2 0.6 copy.17
  135.9 6.6 %adjoint.1 = (f32[128,4]{1,0:T(8,128)}, f32[128,32]{1,0:T(8,128)}) custom-call(s32[1]{0:T(128)} %bitcast.4.me_ref, f32[32,512]{1,0:T(8,128)} %bitcast.13, f32[6,32,40,128]{3,2,1,0:T(8,128)} %get-tuple-element.18.level_ref, f32[5,32,8,128]{3,2,1,0:T(8,128)} %get-tuple-element.19.inverse_ref, f32[5,40,128]{2,1,0:T(8,128)} %get-tuple-element.20.column_ref, ...), custom_call_target="tpu_custom_call" | custom-call | flops 10000000 | bytes 8000000 | tf_op jit(solution)/shard_map/adjoint/pallas_call | solution.py:475
  142.4 1.5 %copy.13 = f32[128,4]{0,1:T(4,128)} copy(f32[128,4]{1,0:T(8,128)} %get-tuple-element.31) | data formatting | bytes 4096
  143.9 1.5 %copy.14 = f32[128,32]{0,1:T(8,128)} copy(f32[128,32]{1,0:T(8,128)} %get-tuple-element.32) | data formatting | bytes 32768
  (1 shorter events, 0.0 us)
Async XLA Ops:
  3.1 25.3 %all-to-all-start.1 = ((f32[32,40,128]{2,1,0:T(8,128)}), f32[32,40,128]{2,1,0:T(8,128)S(1)}, u32[]{:S(2)}, u32[]{:S(2)}) async-start(f32[32,40,128]{2,1,0:T(8,128)} %broadcast_in_dim.21), calls=%async_computation.1 | async-start | bytes 1310720 | tf_op jit(solution)/shard_map/all_to_all | solution.py:491
  28.4 3.6 %copy-start = (f32[32,40,128]{2,1,0:T(8,128)}, f32[32,40,128]{2,1,0:T(8,128)S(1)}, u32[]{:S(2)}) copy-start(f32[32,40,128]{2,1,0:T(8,128)S(1)} %all-to-all-done.1.all_ref) | copy-start | bytes 1966084
  28.4 86.1 %all-to-all-start = ((bf16[32,16,3584]{2,1,0:T(8,128)(2,1)}), bf16[32,16,3584]{2,1,0:T(8,128)(2,1)}, u32[]{:S(2)}, u32[]{:S(2)}) async-start(bf16[32,16,3584]{2,1,0:T(8,128)(2,1)} %bitcast.12), calls=%async_computation | async-start | bytes 7340032 | tf_op jit(solution)/shard_map/all_to_all | solution.py:514

commit v2 on v1

--- a/solution.py
+++ b/solution.py
@@ -5,13 +5,15 @@
 from jax import lax
 from jax.experimental import pallas as pl
 from jax.experimental.pallas import tpu as pltpu
+from jax.sharding import Mesh
 from jax.sharding import PartitionSpec as P
 
 ITERS = 5
 SOFTCAP = 4.0
 LANES = 128
 SUBLANES = 8
-AXES = ("group", "expert")
+AXES = ("half", "plane", "expert")
+NEAR = ("plane", "expert")
 REPLICATED_BYTES = 1 << 20
 
 
@@ -72,11 +74,10 @@
 
 
 def distributed(group_logits, expert_logits, expert_ids, cotangent, hidden_saved, w_down):
-    groups = lax.axis_size("group")
+    groups = lax.axis_size(("half", "plane"))
     per_group = lax.axis_size("expert")
     experts = groups * per_group
     tokens_here, top_count = expert_ids.shape
-    model_width = cotangent.shape[1]
     capacity = hidden_saved.shape[1] // experts
     slots = experts * capacity
     targets = (float(tokens_here * per_group), float(tokens_here * groups))
@@ -132,59 +133,75 @@
     return (grad_rows[None], d_group_logits, d_expert_logits)
 
 
-def pack_kernel(ids_ref, rows_ref, out_ref, place_ref, *, experts, capacity):
-    tokens, top_count = ids_ref.shape
-    slots = experts * capacity
+def place_rows(ids, first, experts, capacity):
+    lanes = ids[0].shape[1]
+    expert = lax.broadcasted_iota(jnp.int32, (experts, lanes), 0)
+    hits = [(row - first) == expert for row in ids]
+    picked = sum(hit.astype(jnp.float32) for hit in hits)
+    earlier = (
+        lax.broadcasted_iota(jnp.int32, (lanes, lanes), 0)
+        < lax.broadcasted_iota(jnp.int32, (lanes, lanes), 1)
+    ).astype(jnp.bfloat16)
+    before = jnp.dot(picked.astype(jnp.bfloat16), earlier, preferred_element_type=jnp.float32)
+    slot_of = (expert * capacity).astype(jnp.float32) + before
+    slot_at = lax.broadcasted_iota(jnp.int32, (experts * capacity, lanes), 0)
+    place = jnp.zeros((experts * capacity, lanes), jnp.float32)
+    for row, hit in zip(ids, hits):
+        slot = jnp.sum(jnp.where(hit, slot_of, 0.0), 0, keepdims=True).astype(jnp.int32)
+        here = (row >= first) & (row < first + experts)
+        slot = jnp.where(here, slot, -1)
+        place = place + (slot == slot_at).astype(jnp.float32)
+    return place.astype(jnp.bfloat16)
+
+
+def mine_kernel(group_ref, ids_ref, expert_ref, out_ref):
+    groups, top_count = group_ref.shape[0], ids_ref.shape[0]
+    out_ref[:SUBLANES, :] = jnp.zeros((SUBLANES, out_ref.shape[1]), jnp.float32)
+    out_ref[:groups, :] = group_ref[...]
+    out_ref[groups : groups + top_count, :] = ids_ref[...].astype(jnp.float32)
+    out_ref[SUBLANES:, :] = expert_ref[...]
+
+
+def pack_kernel(small_ref, rows_ref, *refs, near, capacity, first_id, top_count):
+    out_ref, place_ref = refs[-2:]
 
     @pl.when(pl.program_id(0) == 0)
     def _():
-        ids = ids_ref[...]
-        columns = lax.broadcasted_iota(jnp.int32, (tokens, LANES), 1)
-        chosen = [ids[:, k : k + 1] == columns for k in range(top_count)]
-        picked = sum(c.astype(jnp.float32) for c in chosen)
-        row = lax.broadcasted_iota(jnp.int32, (tokens, tokens), 0)
-        column = lax.broadcasted_iota(jnp.int32, (tokens, tokens), 1)
-        earlier = (column < row).astype(jnp.bfloat16)
-        before = jnp.dot(
-            earlier, picked.astype(jnp.bfloat16), preferred_element_type=jnp.float32
-        )
-        slot_at = lax.broadcasted_iota(jnp.int32, (tokens, slots), 1)
-        place = jnp.zeros((tokens, slots), jnp.float32)
-        for k in range(top_count):
-            position = jnp.sum(jnp.where(chosen[k], before, 0.0), 1, keepdims=True)
-            slot = ids[:, k : k + 1] * capacity + position.astype(jnp.int32)
-            place = place + (slot == slot_at).astype(jnp.float32)
-        place_ref[...] = place.astype(jnp.bfloat16)
-
-    out_ref[...] = lax.dot_general(
-        place_ref[...],
-        rows_ref[...],
-        (((0,), (0,)), ((), ())),
-        preferred_element_type=jnp.float32,
+        ids = [
+            small_ref[first_id + k : first_id + k + 1, :].astype(jnp.int32)
+            for k in range(top_count)
+        ]
+        place_ref[...] = place_rows(ids, lax.axis_index("half") * near, near, capacity)
+
+    out_ref[...] = jnp.dot(
+        place_ref[...], rows_ref[...], preferred_element_type=jnp.float32
     ).astype(out_ref.dtype)
 
 
-def pack_rows(expert_ids, cotangent, experts, capacity):
-    tokens, width = cotangent.shape
-    slots = experts * capacity
-    block = 512 if width % 512 == 0 else width
+def pack_rows(small, rows, near, capacity, first_id, top_count, after):
+    tokens, width = rows.shape
+    slots = near * capacity
+    block = max(n for n in range(LANES, 8 * LANES, LANES) if width % n == 0)
     return pl.pallas_call(
-        partial(pack_kernel, experts=experts, capacity=capacity),
-        out_shape=jax.ShapeDtypeStruct((slots, width), cotangent.dtype),
+        partial(
+            pack_kernel, near=near, capacity=capacity, first_id=first_id, top_count=top_count
+        ),
+        out_shape=jax.ShapeDtypeStruct((slots, width), rows.dtype),
         grid=(width // block,),
         in_specs=[
-            pl.BlockSpec(expert_ids.shape, lambda i: (0, 0)),
+            pl.BlockSpec(small.shape, lambda i: (0, 0)),
             pl.BlockSpec((tokens, block), lambda i: (0, i)),
-        ],
+        ]
+        + [pl.BlockSpec(memory_space=pl.ANY)] * len(after),
         out_specs=pl.BlockSpec((slots, block), lambda i: (0, i)),
-        scratch_shapes=[pltpu.VMEM((tokens, slots), jnp.bfloat16)],
+        scratch_shapes=[pltpu.VMEM((slots, tokens), rows.dtype)],
         cost_estimate=pl.CostEstimate(
             flops=2 * tokens * slots * width,
             bytes_accessed=2 * width * (tokens + slots),
             transcendentals=0,
         ),
         name="pack_rows",
-    )(expert_ids, cotangent)
+    )(small, rows, *after)
 
 
 def tile_rows(g):
@@ -192,11 +209,19 @@
 
 
 def forward_kernel(
-    me_ref, all_ref, level_ref, inverse_ref, column_ref, seed_q_ref, seed_p_ref, where_ref,
-    gate_ref, own_ref, dense_ref, before_ref, *, groups, top_count, capacity, targets
+    all_ref, *refs, groups, top_count, capacity, targets, extra
 ):
-    devices = all_ref.shape[0]
+    (level_ref, inverse_ref, column_ref, seed_q_ref, seed_p_ref, where_ref,
+     gate_ref, own_ref, dense_ref, before_ref) = refs[extra:]
+    near, halves = all_ref.shape[:2]
+    devices = near * halves
     tiles = groups + 1
+    half = lax.axis_index("half")
+    inner = lax.axis_index("plane") * lax.axis_size("expert") + lax.axis_index("expert")
+
+    def block(d):
+        return lax.rem(d, near), (lax.div(d, near) != half).astype(jnp.int32)
+
     tile = (SUBLANES, LANES)
     row_id = lax.broadcasted_iota(jnp.int32, tile, 0)
     zero = jnp.zeros(tile, jnp.float32)
@@ -210,14 +235,18 @@
 
     def start(d, sums):
         new = []
+        member, shifted = block(d)
         for i in range(tiles):
             rows = pl.ds(SUBLANES * i, SUBLANES)
-            level = capped(all_ref[d, rows, :])
+            level = capped(all_ref[member, shifted, rows, :])
             if i == 0:
                 level = jnp.where(row_id < groups, level, 0.0)
             level_ref[0, d, rows, :] = level
             new.append(sums[i] + level)
-        named = [all_ref[d, groups + k : groups + k + 1, :].astype(jnp.int32) for k in range(top_count)]
+        named = [
+            all_ref[member, shifted, groups + k : groups + k + 1, :].astype(jnp.int32)
+            for k in range(top_count)
+        ]
         for g in range(groups):
             expert = row_id + g * SUBLANES
             hit = named[0] == expert
@@ -262,7 +291,7 @@
 
     per_block = LANES // capacity
     slot_id = lax.broadcasted_iota(jnp.int32, (capacity, LANES), 0)
-    me = me_ref[0]
+    me = half * near + inner
 
     def finish(d, unused):
         picks = []
@@ -295,11 +324,13 @@
     lax.fori_loop(0, devices, finish, 0)
     for i in range(tiles):
         rows = pl.ds(SUBLANES * i, SUBLANES)
-        own_ref[rows, :] = level_ref[0, me, rows, :] * squashing(all_ref[me, rows, :])
-
-
-def forward(me, everyone, groups, top_count, capacity, targets):
-    devices, rows, lanes = everyone.shape
+        logits = all_ref[inner, 0, rows, :]
+        own_ref[rows, :] = level_ref[0, me, rows, :] * squashing(logits)
+
+
+def forward(everyone, groups, top_count, capacity, targets, after):
+    near, halves, rows, lanes = everyone.shape
+    devices = near * halves
     experts = groups * SUBLANES
     f32 = jnp.float32
     shapes = [
@@ -315,10 +346,15 @@
     vmem = pl.BlockSpec(memory_space=pltpu.VMEM)
     return pl.pallas_call(
         partial(
-            forward_kernel, groups=groups, top_count=top_count, capacity=capacity, targets=targets
+            forward_kernel,
+            groups=groups,
+            top_count=top_count,
+            capacity=capacity,
+            targets=targets,
+            extra=len(after),
         ),
         out_shape=[jax.ShapeDtypeStruct(s, d) for s, d in shapes],
-        in_specs=[pl.BlockSpec(memory_space=pltpu.SMEM), vmem],
+        in_specs=[vmem] + [pl.BlockSpec(memory_space=pl.ANY)] * len(after),
         out_specs=[vmem] * len(shapes),
         scratch_shapes=[
             pltpu.VMEM((devices, experts, lanes), f32),
@@ -326,16 +362,26 @@
         ],
         cost_estimate=pl.CostEstimate(flops=10_000_000, bytes_accessed=8_000_000, transcendentals=0),
         name="forward",
-    )(me, everyone)
-
-
-def product_kernel(rows_ref, weight_ref, saved_ref, gate_ref, grad_ref, slot_ref, sum_ref):
+    )(everyone, *after)
+
+
+def product_kernel(table_ref, *refs, carried, last, extra):
+    refs = list(refs)
+    rows_ref, weight_ref = refs[:2]
+    del refs[:2]
     unscaled = lax.dot_general(
         rows_ref[...],
         weight_ref[...],
         (((1,), (1,)), ((), ())),
         preferred_element_type=jnp.float32,
     )
+    if carried:
+        unscaled = unscaled + refs.pop(0)[...]
+    if not last:
+        refs[extra][...] = unscaled
+        return
+    saved_ref, gate_ref = refs[:2]
+    grad_ref, slot_ref, sum_ref = refs[-3:]
     grad_ref[...] = (gate_ref[:, :1] * unscaled).astype(grad_ref.dtype)
     partial_sums = unscaled * saved_ref[...].astype(jnp.float32)
     folded = partial_sums[:, :LANES]
@@ -353,44 +399,68 @@
 
     @pl.when(pl.program_id(0) == pl.num_programs(0) - 1)
     def _():
-        for j in range(slot_ref.shape[1] // LANES):
-            turned = sum_ref[j * LANES : (j + 1) * LANES, :].T
-            slot_ref[:, j * LANES : (j + 1) * LANES] = jnp.sum(turned, 0, keepdims=True)
-
-
-def product(rows, weight, saved, gates):
+        slot_ref[0] = jnp.sum(sum_ref[...].T, 0, keepdims=True)
+
+
+def product(
+    table, entry, rows, weight, saved, gates, part=0, carried=None, last=True, earlier=None, after=()
+):
     slots, width = rows.shape
     hidden = weight.shape[0]
+    total = saved.shape[0]
     block = 256 if hidden % 256 == 0 else hidden
+    row_block = pl.BlockSpec((slots, block), lambda i, table: (table[entry], i))
+    own_block = pl.BlockSpec((slots, block), lambda i, table: (0, i))
+    operands = [rows, weight]
+    in_specs = [
+        pl.BlockSpec((slots, width), lambda i, table: (0, 0)),
+        pl.BlockSpec((block, width), lambda i, table: (i, part)),
+    ]
+    aliases = {}
+    if carried is not None:
+        operands.append(carried)
+        in_specs.append(own_block)
+    if last:
+        operands += [saved, gates]
+        in_specs += [row_block, pl.BlockSpec((slots, LANES), lambda i, table: (table[entry], 0))]
+        if earlier is not None:
+            aliases = {len(operands) + 1 + i: i for i in range(2)}
+            operands += earlier
+            in_specs += [pl.BlockSpec(memory_space=pl.ANY)] * 2
+        out_shape = [
+            jax.ShapeDtypeStruct((total, hidden), jnp.bfloat16),
+            jax.ShapeDtypeStruct((total // slots, 1, slots), jnp.float32),
+        ]
+        out_specs = [row_block, pl.BlockSpec((1, 1, slots), lambda i, table: (table[entry], 0, 0))]
+        scratch = [pltpu.VMEM((slots, LANES), jnp.float32)]
+    else:
+        out_shape = jax.ShapeDtypeStruct((slots, hidden), jnp.float32)
+        out_specs = own_block
+        scratch = []
+    operands += after
+    in_specs += [pl.BlockSpec(memory_space=pl.ANY)] * len(after)
     return pl.pallas_call(
-        product_kernel,
-        out_shape=[
-            jax.ShapeDtypeStruct((slots, hidden), jnp.bfloat16),
-            jax.ShapeDtypeStruct((1, slots), jnp.float32),
-        ],
-        grid=(hidden // block,),
-        in_specs=[
-            pl.BlockSpec((slots, width), lambda i: (0, 0)),
-            pl.BlockSpec((block, width), lambda i: (i, 0)),
-            pl.BlockSpec((slots, block), lambda i: (0, i)),
-            pl.BlockSpec((slots, LANES), lambda i: (0, 0)),
-        ],
-        out_specs=[
-            pl.BlockSpec((slots, block), lambda i: (0, i)),
-            pl.BlockSpec((1, slots), lambda i: (0, 0)),
-        ],
-        scratch_shapes=[pltpu.VMEM((slots, LANES), jnp.float32)],
+        partial(product_kernel, carried=carried is not None, last=last, extra=len(after)),
+        out_shape=out_shape,
+        grid_spec=pltpu.PrefetchScalarGridSpec(
+            num_scalar_prefetch=1,
+            grid=(hidden // block,),
+            in_specs=in_specs,
+            out_specs=out_specs,
+            scratch_shapes=scratch,
+        ),
+        input_output_aliases=aliases,
         cost_estimate=pl.CostEstimate(
             flops=2 * slots * width * hidden,
             bytes_accessed=2 * (slots * width + hidden * width + 2 * slots * hidden),
             transcendentals=0,
         ),
         name="product",
-    )(rows, weight, saved, gates)
+    )(table, *operands)
 
 
 def adjoint_kernel(
-    me_ref, slot_ref, level_ref, inverse_ref, column_ref, seed_q_ref, seed_p_ref, where_ref,
+    slot_ref, level_ref, inverse_ref, column_ref, seed_q_ref, seed_p_ref, where_ref,
     own_ref, group_ref, expert_ref, carry_ref, *, groups, capacity, targets
 ):
     devices = level_ref.shape[1]
@@ -456,77 +526,104 @@
 
         inner = lax.fori_loop(0, devices, step, (zero,) * tiles, unroll=4)
 
-    me = me_ref[0]
+    me = lax.axis_index(AXES)
     for i, (factor, column) in enumerate(factors_of(0)):
         rows = pl.ds(SUBLANES * i, SUBLANES)
         total = jnp.sum(inner[i], 1, keepdims=True) + zero
         carry_ref[0, rows, :] = (
             factor * (carry_ref[me, rows, :] - total / column) * own_ref[rows, :]
         )
-    turned = carry_ref[0, :, :].T
-    group_ref[...] = turned[:, :groups]
-    expert_ref[...] = turned[:, SUBLANES:]
-
-
-def adjoint(me, slot_grads, saved, own, groups, capacity, targets):
+    group_ref[...] = carry_ref[0, :groups, :]
+    expert_ref[...] = carry_ref[0, SUBLANES:, :]
+
+
+def adjoint(slot_grads, saved, own, groups, capacity, targets):
     level = saved[0]
-    rows, lanes = level.shape[2:]
+    _, lanes = level.shape[2:]
     vmem = pl.BlockSpec(memory_space=pltpu.VMEM)
     return pl.pallas_call(
         partial(adjoint_kernel, groups=groups, capacity=capacity, targets=targets),
         out_shape=[
-            jax.ShapeDtypeStruct((lanes, groups), jnp.float32),
-            jax.ShapeDtypeStruct((lanes, groups * SUBLANES), jnp.float32),
+            jax.ShapeDtypeStruct((groups, lanes), jnp.float32),
+            jax.ShapeDtypeStruct((groups * SUBLANES, lanes), jnp.float32),
         ],
-        in_specs=[pl.BlockSpec(memory_space=pltpu.SMEM)] + [vmem] * (2 + len(saved)),
+        in_specs=[vmem] * (2 + len(saved)),
         out_specs=[vmem, vmem],
         scratch_shapes=[pltpu.VMEM(level.shape[1:], jnp.float32)],
         cost_estimate=pl.CostEstimate(flops=10_000_000, bytes_accessed=8_000_000, transcendentals=0),
         name="adjoint",
-    )(me, slot_grads, *saved, own)
-
-
-def spread(block):
-    copies = jnp.broadcast_to(block[None], (lax.axis_size(AXES),) + block.shape)
-    return lax.all_to_all(copies, AXES, split_axis=0, concat_axis=0)
+    )(slot_grads, *saved, own)
+
+
+def spread(block, axes):
+    copies = jnp.broadcast_to(block[None], (lax.axis_size(axes),) + block.shape)
+    return lax.all_to_all(copies, axes, split_axis=0, concat_axis=0)
 
 
 def replicated(group_logits, expert_logits, expert_ids, cotangent, hidden_saved, w_down):
-    groups = lax.axis_size("group")
+    groups = lax.axis_size(("half", "plane"))
     per_group = lax.axis_size("expert")
+    near = lax.axis_size(NEAR)
     experts = groups * per_group
     tokens_here, top_count = expert_ids.shape
+    width = cotangent.shape[1]
     capacity = hidden_saved.shape[1] // experts
     targets = (float(tokens_here * per_group), float(tokens_here * groups))
-    me = (lax.axis_index("group") * per_group + lax.axis_index("expert")).reshape(1)
-    spare = SUBLANES - groups - top_count
-    mine = jnp.concatenate(
-        [
-            group_logits,
-            expert_ids.astype(jnp.float32),
-            jnp.zeros((tokens_here, spare), jnp.float32),
-            expert_logits,
-        ],
-        1,
-    ).T
-    everyone = spread(mine)
-    send_rows = pack_rows(expert_ids, cotangent, experts, capacity)
-    expert_rows = lax.all_to_all(send_rows, AXES, split_axis=0, concat_axis=0, tiled=True)
-    *saved, gates, own = forward(me, everyone, groups, top_count, capacity, targets)
-    hidden_grad, slot_grad = product(expert_rows, w_down[0], hidden_saved[0], gates)
-    slot_grads = spread(slot_grad).reshape(experts, -1)
-    d_group, d_expert = adjoint(me, slot_grads, saved, own, groups, capacity, targets)
-    return (hidden_grad[None], d_group, d_expert)
+    half = lax.axis_index("half")
+    table = jnp.stack([half, 1 - half]).astype(jnp.int32)
+
+    def swap(block):
+        return lax.ppermute(block, "half", [(0, 1), (1, 0)])
+
+    mine = pl.pallas_call(
+        mine_kernel,
+        out_shape=jax.ShapeDtypeStruct((SUBLANES + experts, tokens_here), jnp.float32),
+        name="mine",
+    )(group_logits.T, expert_ids.T, expert_logits.T)
+    other = swap(mine)
+
+    parts = 2 if width % (2 * LANES) == 0 else 1
+    part = width // parts
+    swapped = []
+    for i in range(parts):
+        block = cotangent[:, i * part : (i + 1) * part]
+        swapped.append(swap(block))
+
+    everyone = spread(jnp.stack([mine, other]), NEAR)
+
+    def send(small, rows, after=()):
+        packed = pack_rows(small, rows, near, capacity, groups, top_count, after)
+        packed = packed.reshape(near, capacity, -1)
+        got = lax.all_to_all(packed, NEAR, split_axis=0, concat_axis=0)
+        return got.reshape(near * capacity, -1)
+
+    weight, hidden = w_down[0], hidden_saved[0]
+    rows = send(mine, cotangent)
+    *saved, gates, own = forward(everyone, groups, top_count, capacity, targets, ())
+    result = product(table, 0, rows, weight, hidden, gates)
+    carried = None
+    for i in range(parts):
+        last = i == parts - 1
+        rows = send(other, swapped[i])
+        carried = product(
+            table, 1, rows, weight, hidden, gates, i, carried, last,
+            list(result) if last else None, () if last else (result[1],),
+        )
+    hidden_grad, slot_grad = carried
+    slot_grads = spread(slot_grad, AXES).reshape(experts, -1)
+    d_group, d_expert = adjoint(slot_grads, saved, own, groups, capacity, targets)
+    return (hidden_grad[None], d_group.T, d_expert.T)
 
 
 def per_device(group_logits, expert_logits, expert_ids, cotangent, hidden_saved, w_down):
-    groups = lax.axis_size("group")
+    groups = lax.axis_size(("half", "plane"))
     per_group = lax.axis_size("expert")
     tokens_here, top_count = expert_ids.shape
     capacity = hidden_saved.shape[1] // (groups * per_group)
     everyone_bytes = 4 * tokens_here * (groups * per_group) * (groups * per_group + SUBLANES)
     fits = (
         tokens_here == LANES
+        and lax.axis_size("half") == 2
         and per_group == SUBLANES
         and groups + top_count <= SUBLANES
         and LANES % capacity == 0
@@ -538,11 +635,14 @@
 
 
 def solution(mesh):
+    groups, per_group = mesh.shape["group"], mesh.shape["expert"]
+    halves = 2 if groups % 2 == 0 else 1
+    parts = Mesh(mesh.devices.reshape(halves, groups // halves, per_group), AXES)
     rows = P(AXES, None)
     blocks = P(AXES, None, None)
     return jax.shard_map(
         per_device,
-        mesh=mesh,
+        mesh=parts,
         in_specs=(rows, rows, rows, rows, blocks, blocks),
         out_specs=(blocks, rows, rows),
         check_vma=False,

time: 146 us -> 161 us (1.10)
  starting transfers between devices: 10.9 us -> 32.7 us
  waiting for transfers between devices: 82.7 us -> 61.5 us
  Pallas kernels: 31.7 us -> 45.8 us
    all_to_all x2 -> x4, waiting for transfers between devices: 82.7 us -> 10.8 us  [the longest x3 10.7 us: send(): got = lax.all_to_all(packed, NEAR, split_axis=0, concat_axis=0)]
    ppermute x0 -> x3, waiting for transfers between devices: none -> 50.7 us  [swap(): return lax.ppermute(block, 'half', [(0, 1), (1, 0)])]
    pallas_call x2 -> x7, Pallas kernels: 15.4 us -> 29.7 us  [the longest x3 19.2 us: product(): pl.pallas_call(partial(product_kernel, carried=carried is not None, last=...]
    all_to_all x2 -> x4, starting transfers between devices: 10.9 us -> 22.5 us  [the longest x3 17.3 us: send(): got = lax.all_to_all(packed, NEAR, split_axis=0, concat_axis=0)]
    ppermute x0 -> x3, starting transfers between devices: none -> 10.3 us  [swap(): return lax.ppermute(block, 'half', [(0, 1), (1, 0)])]
    unnamed x6 -> x16, local copies, waits for them, and re-layouts: 5.04 us -> 4.76 us
  transfers between devices with their start and end apart: 2 -> 7, of which waited for: 2 -> 5; matrix products, arithmetic and copies ran while one was open for 1% -> 1% of each run, Pallas kernels for 11% -> 20%
where the time goes in v2:
time: 161 us; the launch traced here: 160 us
  waiting for transfers between devices  61.5 us (38%)
  Pallas kernels  45.8 us (28%)
  starting transfers between devices  32.7 us (20%)
  blocking collectives  11.3 us (7%)
  local copies, waits for them, and re-layouts  6.92 us (4%)
    ppermute x3, waiting for transfers between devices, swap(): return lax.ppermute(block, 'half', [(0, 1), (1, 0)])  50.7 us
    pallas_call x3, Pallas kernels, product(): pl.pallas_call(partial(product_kernel, carried=carried is not None, last=...  19.2 us
    all_to_all x3, starting transfers between devices, send(): got = lax.all_to_all(packed, NEAR, split_axis=0, concat_axis=0)  17.3 us
    all_to_all x1, blocking collectives, spread(): return lax.all_to_all(copies, axes, split_axis=0, concat_axis=0)  11.3 us
    all_to_all x3, waiting for transfers between devices, send(): got = lax.all_to_all(packed, NEAR, split_axis=0, concat_axis=0)  10.7 us
    ppermute x3, starting transfers between devices, swap(): return lax.ppermute(block, 'half', [(0, 1), (1, 0)])  10.3 us
    pallas_call x1, Pallas kernels, forward(): pl.pallas_call(partial(forward_kernel, groups=groups, top_count=top_count...  9.72 us
    pallas_call x3, Pallas kernels, pack_rows(): pl.pallas_call(partial(pack_kernel, near=near, capacity=capacity, first_i...  9.18 us
  transfers between devices with their start and end apart: 7, of which 5 were waited for; matrix products, arithmetic and copies ran while one was open for 1% of the time, Pallas kernels for 20%

profile of v2, /device:TPU:0, one launch (start us, length us, event | category | flops | bytes accessed | tf_op | source)
XLA Modules:
  0.0 160.3 jit_solution(12816304446924069527)
XLA Ops:
  0.6 1.4 mine.1.small_ref
  2.0 4.1 %collective-permute-start = (f32[40,128]{1,0:T(8,128)}, f32[40,128]{1,0:T(8,128)S(1)}, u32[]{:S(2)}, u32[]{:S(2)}) collective-permute-start(f32[40,128]{1,0:T(8,128)} %mine.1.small_ref), channel_id=1, source_target_pairs={{0,16},{16,0},{1,17},{17,1},{2,18},{18,2},{3,19},{19,3},{4,20},{20... | collective-permute-start | bytes 61448 | tf_op jit(solution)/shard_map/ppermute | solution.py:576
  6.0 2.0 %collective-permute-done.small_ref = f32[40,128]{1,0:T(8,128)S(1)} collective-permute-done((f32[40,128]{1,0:T(8,128)}, f32[40,128]{1,0:T(8,128)S(1)}, u32[]{:S(2)}, u32[]{:S(2)}) %collective-permute-start) | collective-permute-done | bytes 20512 | tf_op jit(solution)/shard_map/ppermute | solution.py:576
  8.0 0.0 copy-start.6
  8.0 0.7 pad_maximum_fusion
  8.8 0.9 broadcast_in_dim.8
  9.7 5.2 %all-to-all-start.3 = ((f32[16,2,40,128]{3,2,1,0:T(8,128)}), f32[16,2,40,128]{3,2,1,0:T(8,128)S(1)}, u32[]{:S(2)}, u32[]{:S(2)}) async-start(f32[16,2,40,128]{3,2,1,0:T(8,128)} %broadcast_in_dim.8), calls=%async_computation.3 | async-start | bytes 1310720 | tf_op jit(solution)/shard_map/all_to_all | solution.py:560
  14.9 1.2 fusion
  16.1 2.8 %collective-permute-start.2 = (bf16[128,1792]{1,0:T(8,128)(2,1)S(1)}, bf16[128,1792]{1,0:T(8,128)(2,1)S(1)}, u32[]{:S(2)}, u32[]{:S(2)}) collective-permute-start(bf16[128,1792]{1,0:T(8,128)(2,1)S(1)} %get-tuple-element.31), channel_id=1, source_target_pairs={{0,16},{16,0},{1,17},{17,1},{2,18},{18,2},{3,19},{19,3},{4,20},{20... | collective-permute-start | bytes 1376264 | tf_op jit(solution)/shard_map/ppermute | solution.py:576
  18.8 21.0 %collective-permute-done.2.rows_ref = bf16[128,1792]{1,0:T(8,128)(2,1)S(1)} collective-permute-done((bf16[128,1792]{1,0:T(8,128)(2,1)S(1)}, bf16[128,1792]{1,0:T(8,128)(2,1)S(1)}, u32[]{:S(2)}, u32[]{:S(2)}) %collective-permute-start.2) | collective-permute-done | bytes 458784 | tf_op jit(solution)/shard_map/ppermute | solution.py:576
  39.8 0.0 copy-done.6
  39.8 0.0 copy-start.5
  39.8 0.8 copy-done.5
  40.6 2.5 %pack_rows.4 = bf16[256,1792]{1,0:T(8,128)(2,1)} custom-call(f32[40,128]{1,0:T(8,128)} %copy-done.6, bf16[128,1792]{1,0:T(8,128)(2,1)} %copy-done.5), custom_call_target="tpu_custom_call" | custom-call | flops 117440512 | bytes 1376256 | tf_op jit(solution)/shard_map/pack_rows/pallas_call | solution.py:185
  43.1 0.0 all-to-all-done.3.all_ref
  43.1 0.0 copy-start.3
  43.1 4.1 %all-to-all-start.1 = ((bf16[16,16,1792]{2,1,0:T(8,128)(2,1)}), bf16[16,16,1792]{2,1,0:T(8,128)(2,1)S(1)}, u32[]{:S(2)}, u32[]{:S(2)}) async-start(bf16[16,16,1792]{2,1,0:T(8,128)(2,1)} %bitcast.34), calls=%async_computation.1 | async-start | bytes 1835008 | tf_op jit(solution)/shard_map/all_to_all | solution.py:597
  47.1 4.2 %pack_rows.5 = bf16[256,3584]{1,0:T(8,128)(2,1)} custom-call(f32[40,128]{1,0:T(8,128)} %mine.1.small_ref, bf16[128,3584]{1,0:T(8,128)(2,1)} %rows_ref.1), custom_call_target="tpu_custom_call" | custom-call | flops 234881024 | bytes 2752512 | tf_op jit(solution)/shard_map/pack_rows/pallas_call | solution.py:185
  51.4 10.5 %all-to-all-done.1 = bf16[16,16,1792]{2,1,0:T(8,128)(2,1)S(1)} async-done(((bf16[16,16,1792]{2,1,0:T(8,128)(2,1)}), bf16[16,16,1792]{2,1,0:T(8,128)(2,1)S(1)}, u32[]{:S(2)}, u32[]{:S(2)}) %all-to-all-start.1) | async-done | bytes 917536 | tf_op jit(solution)/shard_map/all_to_all | solution.py:597
  61.9 0.0 copy-start.2
  61.9 0.9 copy-done.2
  62.8 0.0 copy-done.3
  62.8 3.7 %all-to-all-start.2 = ((bf16[16,16,3584]{2,1,0:T(8,128)(2,1)}), bf16[16,16,3584]{2,1,0:T(8,128)(2,1)S(1)}, u32[]{:S(2)}, u32[]{:S(2)}) async-start(bf16[16,16,3584]{2,1,0:T(8,128)(2,1)} %bitcast.28), calls=%async_computation.2 | async-start | bytes 3670016 | tf_op jit(solution)/shard_map/all_to_all | solution.py:597
  66.5 3.4 %collective-permute-start.1 = (bf16[128,1792]{1,0:T(8,128)(2,1)S(1)}, bf16[128,1792]{1,0:T(8,128)(2,1)S(1)}, u32[]{:S(2)}, u32[]{:S(2)}) collective-permute-start(bf16[128,1792]{1,0:T(8,128)(2,1)S(1)} %get-tuple-element.32), channel_id=1, source_target_pairs={{0,16},{16,0},{1,17},{17,1},{2,18},{18,2},{3,19},{19,3},{4,20},{20... | collective-permute-start | bytes 1376264 | tf_op jit(solution)/shard_map/ppermute | solution.py:576
  70.0 27.8 %collective-permute-done.1.rows_ref = bf16[128,1792]{1,0:T(8,128)(2,1)S(1)} collective-permute-done((bf16[128,1792]{1,0:T(8,128)(2,1)S(1)}, bf16[128,1792]{1,0:T(8,128)(2,1)S(1)}, u32[]{:S(2)}, u32[]{:S(2)}) %collective-permute-start.1) | collective-permute-done | bytes 458784 | tf_op jit(solution)/shard_map/ppermute | solution.py:576
  97.7 0.0 copy-start.4
  97.7 0.8 copy-done.4
  98.5 2.5 %pack_rows.3 = bf16[256,1792]{1,0:T(8,128)(2,1)} custom-call(f32[40,128]{1,0:T(8,128)} %copy-done.6, bf16[128,1792]{1,0:T(8,128)(2,1)} %copy-done.4), custom_call_target="tpu_custom_call" | custom-call | flops 117440512 | bytes 1376256 | tf_op jit(solution)/shard_map/pack_rows/pallas_call | solution.py:185
  101.0 0.3 all-to-all-done.2
  101.3 0.0 copy-start
  101.3 9.5 %all-to-all-start = ((bf16[16,16,1792]{2,1,0:T(8,128)(2,1)}), bf16[16,16,1792]{2,1,0:T(8,128)(2,1)S(1)}, u32[]{:S(2)}, u32[]{:S(2)}) async-start(bf16[16,16,1792]{2,1,0:T(8,128)(2,1)} %bitcast.33), calls=%async_computation | async-start | bytes 1835008 | tf_op jit(solution)/shard_map/all_to_all | solution.py:597
  110.8 0.6 pad_add_fusion.table_ref
  111.4 9.7 %forward.1 = (f32[6,32,40,128]{3,2,1,0:T(8,128)}, f32[5,32,8,128]{3,2,1,0:T(8,128)}, f32[5,40,128]{2,1,0:T(8,128)}, f32[32,32,128]{2,1,0:T(8,128)}, f32[32,32,12...) custom-call(f32[16,2,40,128]{3,2,1,0:T(8,128)} %copy-done.3), custom_call_target="tpu_custom_call" | custom-call | flops 10000000 | bytes 8000000 | tf_op jit(solution)/shard_map/forward/pallas_call | solution.py:347
  121.1 0.0 copy-done
  121.1 7.4 %product.3 = (bf16[512,1024]{1,0:T(8,128)(2,1)}, f32[2,1,256]{2,1,0:T(1,128)}) custom-call(s32[2]{0:T(128)} %pad_add_fusion.table_ref, bf16[256,3584]{1,0:T(8,128)(2,1)} %bitcast.29, bf16[1024,3584]{1,0:T(8,128)(2,1)} %bitcast.25, bf16[512,1024]{1,0:T(8,128)(2,1)} %bitcast.30, f32[512,128]{1,0:T(8,128)} %get-tuple-element.17.refs_3_.refs_4_), custom_call_target="tpu_custom_call" | custom-call | flops 1879048192 | bytes 10223616 | tf_op jit(solution)/shard_map/product/pallas_call | solution.py:442
  128.5 5.7 %product.4.refs_2_ = f32[256,1024]{1,0:T(8,128)} custom-call(s32[2]{0:T(128)} %pad_add_fusion.table_ref, bf16[256,1792]{1,0:T(8,128)(2,1)} %bitcast.35, bf16[1024,3584]{1,0:T(8,128)(2,1)} %bitcast.26, f32[2,1,256]{2,1,0:T(1,128)} %get-tuple-element.18.refs_2_.refs_6_), custom_call_target="tpu_custom_call" | custom-call | flops 939524096 | bytes 5636096 | tf_op jit(solution)/shard_map/product/pallas_call | solution.py:442
  134.2 0.0 all-to-all-done
  134.2 0.0 copy-start.1
  134.2 1.0 copy-done.1
  135.2 6.1 %product.5 = (bf16[512,1024]{1,0:T(8,128)(2,1)}, f32[2,1,256]{2,1,0:T(1,128)}) custom-call(s32[2]{0:T(128)} %pad_add_fusion.table_ref, bf16[256,1792]{1,0:T(8,128)(2,1)} %bitcast.32, bf16[1024,3584]{1,0:T(8,128)(2,1)} %bitcast.27, f32[256,1024]{1,0:T(8,128)} %product.4.refs_2_, ...), custom_call_target="tpu_custom_call", output_to_operand_aliasing={{0}: (6, {}), {1}: (7, {})} | custom-call | flops 939524096 | bytes 5636096 | tf_op jit(solution)/shard_map/product/pallas_call | solution.py:442
  141.3 0.7 copy.14
  142.0 11.3 %all_to_all.25 = f32[32,2,1,256]{3,1,2,0:T(2,128)S(1)} all-to-all(f32[32,2,1,256]{3,1,2,0:T(2,128)S(1)} %broadcast_in_dim.20), channel_id=1, replica_groups=mesh['half'=2,'plane'=2,'expert'=8] {'half','plane','expert'}, dimensions={0} | all-to-all | bytes 131072 | tf_op jit(solution)/shard_map/all_to_all | solution.py:560
  153.3 0.6 copy.12
  153.9 6.4 %adjoint.1 = (f32[4,128]{1,0:T(4,128)}, f32[32,128]{1,0:T(8,128)}) custom-call(f32[32,512]{1,0:T(8,128)} %bitcast.37, f32[6,32,40,128]{3,2,1,0:T(8,128)} %get-tuple-element.22.level_ref, f32[5,32,8,128]{3,2,1,0:T(8,128)} %get-tuple-element.23.inverse_ref, f32[5,40,128]{2,1,0:T(8,128)} %get-tuple-element.24.column_ref, ...), custom_call_target="tpu_custom_call" | custom-call | flops 10000000 | bytes 8000000 | tf_op jit(solution)/shard_map/adjoint/pallas_call | solution.py:544
  (1 shorter events, 0.0 us)
Async XLA Ops:
  2.0 6.0 %collective-permute-start = (f32[40,128]{1,0:T(8,128)}, f32[40,128]{1,0:T(8,128)S(1)}, u32[]{:S(2)}, u32[]{:S(2)}) collective-permute-start(f32[40,128]{1,0:T(8,128)} %mine.1.small_ref), channel_id=1, source_target_pairs={{0,16},{16,0},{1,17},{17,1},{2,18},{18,2},{3,19},{19,3},{4,20},{20... | collective-permute-start | bytes 61448 | tf_op jit(solution)/shard_map/ppermute | solution.py:576
  8.0 31.8 %copy-start.6 = (f32[40,128]{1,0:T(8,128)}, f32[40,128]{1,0:T(8,128)S(1)}, u32[]{:S(2)}) copy-start(f32[40,128]{1,0:T(8,128)S(1)} %collective-permute-done.small_ref) | copy-start | bytes 61444
  9.7 33.4 %all-to-all-start.3 = ((f32[16,2,40,128]{3,2,1,0:T(8,128)}), f32[16,2,40,128]{3,2,1,0:T(8,128)S(1)}, u32[]{:S(2)}, u32[]{:S(2)}) async-start(f32[16,2,40,128]{3,2,1,0:T(8,128)} %broadcast_in_dim.8), calls=%async_computation.3 | async-start | bytes 1310720 | tf_op jit(solution)/shard_map/all_to_all | solution.py:560
  16.1 23.7 %collective-permute-start.2 = (bf16[128,1792]{1,0:T(8,128)(2,1)S(1)}, bf16[128,1792]{1,0:T(8,128)(2,1)S(1)}, u32[]{:S(2)}, u32[]{:S(2)}) collective-permute-start(bf16[128,1792]{1,0:T(8,128)(2,1)S(1)} %get-tuple-element.31), channel_id=1, source_target_pairs={{0,16},{16,0},{1,17},{17,1},{2,18},{18,2},{3,19},{19,3},{4,20},{20... | collective-permute-start | bytes 1376264 | tf_op jit(solution)/shard_map/ppermute | solution.py:576
  39.8 0.8 copy-start.5
  43.1 19.7 %copy-start.3 = (f32[16,2,40,128]{3,2,1,0:T(8,128)}, f32[16,2,40,128]{3,2,1,0:T(8,128)S(1)}, u32[]{:S(2)}) copy-start(f32[16,2,40,128]{3,2,1,0:T(8,128)S(1)} %all-to-all-done.3.all_ref) | copy-start | bytes 1966084
  43.1 18.8 %all-to-all-start.1 = ((bf16[16,16,1792]{2,1,0:T(8,128)(2,1)}), bf16[16,16,1792]{2,1,0:T(8,128)(2,1)S(1)}, u32[]{:S(2)}, u32[]{:S(2)}) async-start(bf16[16,16,1792]{2,1,0:T(8,128)(2,1)} %bitcast.34), calls=%async_computation.1 | async-start | bytes 1835008 | tf_op jit(solution)/shard_map/all_to_all | solution.py:597
  61.9 0.9 copy-start.2
  62.8 38.5 %all-to-all-start.2 = ((bf16[16,16,3584]{2,1,0:T(8,128)(2,1)}), bf16[16,16,3584]{2,1,0:T(8,128)(2,1)S(1)}, u32[]{:S(2)}, u32[]{:S(2)}) async-start(bf16[16,16,3584]{2,1,0:T(8,128)(2,1)} %bitcast.28), calls=%async_computation.2 | async-start | bytes 3670016 | tf_op jit(solution)/shard_map/all_to_all | solution.py:597
  66.5 31.2 %collective-permute-start.1 = (bf16[128,1792]{1,0:T(8,128)(2,1)S(1)}, bf16[128,1792]{1,0:T(8,128)(2,1)S(1)}, u32[]{:S(2)}, u32[]{:S(2)}) collective-permute-start(bf16[128,1792]{1,0:T(8,128)(2,1)S(1)} %get-tuple-element.32), channel_id=1, source_target_pairs={{0,16},{16,0},{1,17},{17,1},{2,18},{18,2},{3,19},{19,3},{4,20},{20... | collective-permute-start | bytes 1376264 | tf_op jit(solution)/shard_map/ppermute | solution.py:576
  97.7 0.8 copy-start.4
  101.3 19.9 %copy-start = (bf16[16,16,3584]{2,1,0:T(8,128)(2,1)}, bf16[16,16,3584]{2,1,0:T(8,128)(2,1)S(1)}, u32[]{:S(2)}) copy-start(bf16[16,16,3584]{2,1,0:T(8,128)(2,1)S(1)} %all-to-all-done.2) | copy-start | bytes 5505028
  101.3 33.0 %all-to-all-start = ((bf16[16,16,1792]{2,1,0:T(8,128)(2,1)}), bf16[16,16,1792]{2,1,0:T(8,128)(2,1)S(1)}, u32[]{:S(2)}, u32[]{:S(2)}) async-start(bf16[16,16,1792]{2,1,0:T(8,128)(2,1)} %bitcast.33), calls=%async_computation | async-start | bytes 1835008 | tf_op jit(solution)/shard_map/all_to_all | solution.py:597
  134.2 1.0 copy-start.1

commit v3 on v2

--- a/solution.py
+++ b/solution.py
@@ -162,8 +162,8 @@
     out_ref[SUBLANES:, :] = expert_ref[...]
 
 
-def pack_kernel(small_ref, rows_ref, *refs, near, capacity, first_id, top_count):
-    out_ref, place_ref = refs[-2:]
+def pack_kernel(small_ref, *refs, near, capacity, first_id, top_count):
+    *rows_refs, out_ref, place_ref = refs
 
     @pl.when(pl.program_id(0) == 0)
     def _():
@@ -173,35 +173,36 @@
         ]
         place_ref[...] = place_rows(ids, lax.axis_index("half") * near, near, capacity)
 
+    rows = rows_refs[0][...]
+    for rows_ref in rows_refs[1:]:
+        rows = rows + rows_ref[...]
     out_ref[...] = jnp.dot(
-        place_ref[...], rows_ref[...], preferred_element_type=jnp.float32
+        place_ref[...], rows, preferred_element_type=jnp.float32
     ).astype(out_ref.dtype)
 
 
-def pack_rows(small, rows, near, capacity, first_id, top_count, after):
-    tokens, width = rows.shape
+def pack_rows(small, rows, near, capacity, first_id, top_count):
+    tokens, width = rows[0].shape
+    dtype = rows[0].dtype
     slots = near * capacity
     block = max(n for n in range(LANES, 8 * LANES, LANES) if width % n == 0)
     return pl.pallas_call(
         partial(
             pack_kernel, near=near, capacity=capacity, first_id=first_id, top_count=top_count
         ),
-        out_shape=jax.ShapeDtypeStruct((slots, width), rows.dtype),
+        out_shape=jax.ShapeDtypeStruct((slots, width), dtype),
         grid=(width // block,),
-        in_specs=[
-            pl.BlockSpec(small.shape, lambda i: (0, 0)),
-            pl.BlockSpec((tokens, block), lambda i: (0, i)),
-        ]
-        + [pl.BlockSpec(memory_space=pl.ANY)] * len(after),
+        in_specs=[pl.BlockSpec(small.shape, lambda i: (0, 0))]
+        + [pl.BlockSpec((tokens, block), lambda i: (0, i))] * len(rows),
         out_specs=pl.BlockSpec((slots, block), lambda i: (0, i)),
-        scratch_shapes=[pltpu.VMEM((slots, tokens), rows.dtype)],
+        scratch_shapes=[pltpu.VMEM((slots, tokens), dtype)],
         cost_estimate=pl.CostEstimate(
             flops=2 * tokens * slots * width,
             bytes_accessed=2 * width * (tokens + slots),
             transcendentals=0,
         ),
         name="pack_rows",
-    )(small, rows, *after)
+    )(small, *rows)
 
 
 def tile_rows(g):
@@ -209,18 +210,21 @@
 
 
 def forward_kernel(
-    all_ref, *refs, groups, top_count, capacity, targets, extra
+    all_ref, *refs, groups, top_count, capacity, targets, cube
 ):
     (level_ref, inverse_ref, column_ref, seed_q_ref, seed_p_ref, where_ref,
-     gate_ref, own_ref, dense_ref, before_ref) = refs[extra:]
-    near, halves = all_ref.shape[:2]
-    devices = near * halves
+     gate_ref, own_ref, dense_ref, before_ref) = refs
+    devices = all_ref.shape[0]
     tiles = groups + 1
-    half = lax.axis_index("half")
-    inner = lax.axis_index("plane") * lax.axis_size("expert") + lax.axis_index("expert")
+    me = lax.axis_index(AXES)
 
     def block(d):
-        return lax.rem(d, near), (lax.div(d, near) != half).astype(jnp.int32)
+        across = jnp.bitwise_xor(d, me)
+        place = jnp.int32(0)
+        for step, bit in enumerate(cube):
+            flag = jnp.bitwise_and(lax.shift_right_logical(across, jnp.int32(bit)), 1)
+            place = place + flag * (1 << step)
+        return place
 
     tile = (SUBLANES, LANES)
     row_id = lax.broadcasted_iota(jnp.int32, tile, 0)
@@ -235,16 +239,16 @@
 
     def start(d, sums):
         new = []
-        member, shifted = block(d)
+        place = block(d)
         for i in range(tiles):
             rows = pl.ds(SUBLANES * i, SUBLANES)
-            level = capped(all_ref[member, shifted, rows, :])
+            level = capped(all_ref[place, rows, :])
             if i == 0:
                 level = jnp.where(row_id < groups, level, 0.0)
             level_ref[0, d, rows, :] = level
             new.append(sums[i] + level)
         named = [
-            all_ref[member, shifted, groups + k : groups + k + 1, :].astype(jnp.int32)
+            all_ref[place, groups + k : groups + k + 1, :].astype(jnp.int32)
             for k in range(top_count)
         ]
         for g in range(groups):
@@ -291,7 +295,6 @@
 
     per_block = LANES // capacity
     slot_id = lax.broadcasted_iota(jnp.int32, (capacity, LANES), 0)
-    me = half * near + inner
 
     def finish(d, unused):
         picks = []
@@ -324,13 +327,12 @@
     lax.fori_loop(0, devices, finish, 0)
     for i in range(tiles):
         rows = pl.ds(SUBLANES * i, SUBLANES)
-        logits = all_ref[inner, 0, rows, :]
+        logits = all_ref[0, rows, :]
         own_ref[rows, :] = level_ref[0, me, rows, :] * squashing(logits)
 
 
-def forward(everyone, groups, top_count, capacity, targets, after):
-    near, halves, rows, lanes = everyone.shape
-    devices = near * halves
+def forward(everyone, cube, groups, top_count, capacity, targets):
+    devices, rows, lanes = everyone.shape
     experts = groups * SUBLANES
     f32 = jnp.float32
     shapes = [
@@ -351,10 +353,10 @@
             top_count=top_count,
             capacity=capacity,
             targets=targets,
-            extra=len(after),
+            cube=cube,
         ),
         out_shape=[jax.ShapeDtypeStruct(s, d) for s, d in shapes],
-        in_specs=[vmem] + [pl.BlockSpec(memory_space=pl.ANY)] * len(after),
+        in_specs=[vmem],
         out_specs=[vmem] * len(shapes),
         scratch_shapes=[
             pltpu.VMEM((devices, experts, lanes), f32),
@@ -362,7 +364,7 @@
         ],
         cost_estimate=pl.CostEstimate(flops=10_000_000, bytes_accessed=8_000_000, transcendentals=0),
         name="forward",
-    )(everyone, *after)
+    )(everyone)
 
 
 def product_kernel(table_ref, *refs, carried, last, extra):
@@ -560,56 +562,59 @@
     return lax.all_to_all(copies, axes, split_axis=0, concat_axis=0)
 
 
+def cube_bits(groups, per_group):
+    low = per_group.bit_length() - 1
+    high = (groups * per_group).bit_length() - 1
+    return [*range(low, high), *range(low)]
+
+
 def replicated(group_logits, expert_logits, expert_ids, cotangent, hidden_saved, w_down):
     groups = lax.axis_size(("half", "plane"))
     per_group = lax.axis_size("expert")
     near = lax.axis_size(NEAR)
     experts = groups * per_group
     tokens_here, top_count = expert_ids.shape
-    width = cotangent.shape[1]
     capacity = hidden_saved.shape[1] // experts
     targets = (float(tokens_here * per_group), float(tokens_here * groups))
     half = lax.axis_index("half")
     table = jnp.stack([half, 1 - half]).astype(jnp.int32)
 
-    def swap(block):
-        return lax.ppermute(block, "half", [(0, 1), (1, 0)])
+    planes = lax.axis_size("plane")
 
     mine = pl.pallas_call(
         mine_kernel,
         out_shape=jax.ShapeDtypeStruct((SUBLANES + experts, tokens_here), jnp.float32),
         name="mine",
     )(group_logits.T, expert_ids.T, expert_logits.T)
-    other = swap(mine)
-
-    parts = 2 if width % (2 * LANES) == 0 else 1
-    part = width // parts
+    column = [mine]
+    for across in range(1, groups):
+        pairs = [(d, d ^ (across * per_group)) for d in range(experts)]
+        column.append(lax.ppermute(mine, AXES, pairs))
+    other = column[planes]
+    cube = cube_bits(groups, per_group)
+    everyone = jnp.stack(column)
+    for bit in cube[groups.bit_length() - 1 :]:
+        pairs = [(d, d ^ (1 << bit)) for d in range(experts)]
+        everyone = jnp.concatenate([everyone, lax.ppermute(everyone, AXES, pairs)])
+
     swapped = []
-    for i in range(parts):
-        block = cotangent[:, i * part : (i + 1) * part]
-        swapped.append(swap(block))
-
-    everyone = spread(jnp.stack([mine, other]), NEAR)
-
-    def send(small, rows, after=()):
-        packed = pack_rows(small, rows, near, capacity, groups, top_count, after)
+    for j in range(planes):
+        up, down = (j, j + planes), (2 * planes - 1 - j, planes - 1 - j)
+        swapped.append(lax.ppermute(cotangent, ("half", "plane"), [up, down]))
+
+    def send(small, rows):
+        packed = pack_rows(small, rows, near, capacity, groups, top_count)
         packed = packed.reshape(near, capacity, -1)
         got = lax.all_to_all(packed, NEAR, split_axis=0, concat_axis=0)
         return got.reshape(near * capacity, -1)
 
     weight, hidden = w_down[0], hidden_saved[0]
-    rows = send(mine, cotangent)
-    *saved, gates, own = forward(everyone, groups, top_count, capacity, targets, ())
-    result = product(table, 0, rows, weight, hidden, gates)
-    carried = None
-    for i in range(parts):
-        last = i == parts - 1
-        rows = send(other, swapped[i])
-        carried = product(
-            table, 1, rows, weight, hidden, gates, i, carried, last,
-            list(result) if last else None, () if last else (result[1],),
-        )
-    hidden_grad, slot_grad = carried
+    own_rows = send(mine, [cotangent])
+    other_rows = send(other, swapped)
+    *saved, gates, own = forward(everyone, cube, groups, top_count, capacity, targets)
+    result = product(table, 0, own_rows, weight, hidden, gates)
+    result = product(table, 1, other_rows, weight, hidden, gates, earlier=list(result))
+    hidden_grad, slot_grad = result
     slot_grads = spread(slot_grad, AXES).reshape(experts, -1)
     d_group, d_expert = adjoint(slot_grads, saved, own, groups, capacity, targets)
     return (hidden_grad[None], d_group.T, d_expert.T)
@@ -623,7 +628,7 @@
     everyone_bytes = 4 * tokens_here * (groups * per_group) * (groups * per_group + SUBLANES)
     fits = (
         tokens_here == LANES
-        and lax.axis_size("half") == 2
+        and groups in (2, 4)
         and per_group == SUBLANES
         and groups + top_count <= SUBLANES
         and LANES % capacity == 0

time: 161 us -> 162 us (level)
  waiting for transfers between devices: 61.5 us -> 75.8 us
  starting transfers between devices: 32.7 us -> 27.9 us
  Pallas kernels: 45.8 us -> 41.1 us
  blocking collectives: 11.3 us -> 9.64 us
    ppermute x3 -> x8, waiting for transfers between devices: 50.7 us -> 75.8 us  [the longest x3 62.4 us: replicated(): column.append(lax.ppermute(mine, AXES, pairs))]
    all_to_all x3 -> x2, waiting for transfers between devices: 10.7 us -> 0.01 us  [send(): got = lax.all_to_all(packed, NEAR, split_axis=0, concat_axis=0)]
    ppermute x3 -> x8, starting transfers between devices: 10.3 us -> 17.5 us  [the longest x3 7.08 us: replicated(): column.append(lax.ppermute(mine, AXES, pairs))]
    all_to_all x3 -> x2, starting transfers between devices: 17.3 us -> 10.4 us  [send(): got = lax.all_to_all(packed, NEAR, split_axis=0, concat_axis=0)]
    all_to_all x1 -> x0, starting transfers between devices: 5.16 us -> none  [spread(): return lax.all_to_all(copies, axes, split_axis=0, concat_axis=0)]
    pallas_call x3 -> x2, Pallas kernels: 19.2 us -> 14.8 us  [product(): pl.pallas_call(partial(product_kernel, carried=carried is not None, last=...]
    all_to_all x1, blocking collectives: 11.3 us -> 9.64 us  [spread(): return lax.all_to_all(copies, axes, split_axis=0, concat_axis=0)]
    unnamed x16 -> x21, local copies, waits for them, and re-layouts: 4.76 us -> 5.6 us
  transfers between devices with their start and end apart: 7 -> 10, of which waited for: 5 -> 5; matrix products, arithmetic and copies ran while one was open for 1% -> 0% of each run, Pallas kernels for 20% -> 13%
where the time goes in v3:
time: 162 us; the launch traced here: 161 us
  waiting for transfers between devices  75.8 us (47%)
  Pallas kernels  41.1 us (25%)
  starting transfers between devices  27.9 us (17%)
  blocking collectives  9.64 us (6%)
  local copies, waits for them, and re-layouts  5.66 us (3%)
    ppermute x3, waiting for transfers between devices, replicated(): column.append(lax.ppermute(mine, AXES, pairs))  62.4 us
    pallas_call x2, Pallas kernels, product(): pl.pallas_call(partial(product_kernel, carried=carried is not None, last=...  14.8 us
    ppermute x3, waiting for transfers between devices, replicated(): everyone = jnp.concatenate([everyone, lax.ppermute(everyone, AXES, pairs)])  13.4 us
    all_to_all x2, starting transfers between devices, send(): got = lax.all_to_all(packed, NEAR, split_axis=0, concat_axis=0)  10.4 us
    pallas_call x1, Pallas kernels, forward(): pl.pallas_call(partial(forward_kernel, groups=groups, top_count=top_count...  9.86 us
    all_to_all x1, blocking collectives, spread(): return lax.all_to_all(copies, axes, split_axis=0, concat_axis=0)  9.64 us
    pallas_call x2, Pallas kernels, pack_rows(): pl.pallas_call(partial(pack_kernel, near=near, capacity=capacity, first_i...  8.71 us
    ppermute x3, starting transfers between devices, replicated(): column.append(lax.ppermute(mine, AXES, pairs))  7.08 us
  transfers between devices with their start and end apart: 10, of which 5 were waited for; matrix products, arithmetic and copies ran while one was open for 0% of the time, Pallas kernels for 13%

profile of v3, /device:TPU:0, one launch (start us, length us, event | category | flops | bytes accessed | tf_op | source)
XLA Modules:
  0.0 161.4 jit_solution(5552391303887994771)
XLA Ops:
  0.6 1.4 mine.1.small_ref
  2.0 4.2 %pack_rows.3 = bf16[256,3584]{1,0:T(8,128)(2,1)} custom-call(f32[40,128]{1,0:T(8,128)} %mine.1.small_ref, bf16[128,3584]{1,0:T(8,128)(2,1)} %refs_0_.1), custom_call_target="tpu_custom_call" | custom-call | flops 234881024 | bytes 2752512 | tf_op jit(solution)/shard_map/pack_rows/pallas_call | solution.py:189
  6.2 0.0 copy-start.4
  6.2 6.4 %all-to-all-start.1 = ((bf16[16,16,3584]{2,1,0:T(8,128)(2,1)}), bf16[16,16,3584]{2,1,0:T(8,128)(2,1)S(1)}, u32[]{:S(2)}, u32[]{:S(2)}) async-start(bf16[16,16,3584]{2,1,0:T(8,128)(2,1)} %bitcast.41), calls=%async_computation.1 | async-start | bytes 3670016 | tf_op jit(solution)/shard_map/all_to_all | solution.py:608
  12.7 4.6 %collective-permute-start.1 = (bf16[128,3584]{1,0:T(8,128)(2,1)}, bf16[128,3584]{1,0:T(8,128)(2,1)S(1)}, u32[]{:S(2)}, u32[]{:S(2)}) collective-permute-start(bf16[128,3584]{1,0:T(8,128)(2,1)} %refs_0_.1), channel_id=1, source_target_pairs={{0,16},{24,8},{1,17},{25,9},{2,18},{26,10},{3,19},{27,11},{4,20},{... | collective-permute-start | bytes 2752520 | tf_op jit(solution)/shard_map/ppermute | solution.py:603
  17.2 1.3 collective-permute-start.2
  18.5 0.0 copy-done.4
  18.5 4.5 %collective-permute-start = (f32[40,128]{1,0:T(8,128)S(1)}, f32[40,128]{1,0:T(8,128)S(1)}, u32[]{:S(2)}, u32[]{:S(2)}) collective-permute-start(f32[40,128]{1,0:T(8,128)S(1)} %copy-done.4), channel_id=1, source_target_pairs={{0,16},{1,17},{2,18},{3,19},{4,20},{5,21},{6,22},{7,23},{8,24},{9,... | collective-permute-start | bytes 61448 | tf_op jit(solution)/shard_map/ppermute | solution.py:592
  23.0 40.2 %collective-permute-done.small_ref = f32[40,128]{1,0:T(8,128)S(1)} collective-permute-done((f32[40,128]{1,0:T(8,128)S(1)}, f32[40,128]{1,0:T(8,128)S(1)}, u32[]{:S(2)}, u32[]{:S(2)}) %collective-permute-start) | collective-permute-done | bytes 20512 | tf_op jit(solution)/shard_map/ppermute | solution.py:592
  63.2 0.0 copy-start.5
  63.2 0.0 collective-permute-done.1.refs_0_
  63.2 0.0 copy-start.2
  63.2 0.0 collective-permute-done.2.refs_1_
  63.2 0.6 copy-done.5
  63.8 0.3 copy-done.2
  64.1 4.5 %pack_rows.2 = bf16[256,3584]{1,0:T(8,128)(2,1)} custom-call(f32[40,128]{1,0:T(8,128)} %copy-done.5, bf16[128,3584]{1,0:T(8,128)(2,1)} %copy-done.2, bf16[128,3584]{1,0:T(8,128)(2,1)} %collective-permute-done.2.refs_1_), custom_call_target="tpu_custom_call" | custom-call | flops 234881024 | bytes 2752512 | tf_op jit(solution)/shard_map/pack_rows/pallas_call | solution.py:189
  68.6 0.0 all-to-all-done.1
  68.6 0.0 copy-start.1
  68.6 0.0 copy-start.6
  68.6 1.2 copy-done.1
  69.9 3.9 %all-to-all-start = ((bf16[16,16,3584]{2,1,0:T(8,128)(2,1)}), bf16[16,16,3584]{2,1,0:T(8,128)(2,1)S(1)}, u32[]{:S(2)}, u32[]{:S(2)}) async-start(bf16[16,16,3584]{2,1,0:T(8,128)(2,1)} %bitcast.40), calls=%async_computation | async-start | bytes 3670016 | tf_op jit(solution)/shard_map/all_to_all | solution.py:608
  73.8 2.6 %collective-permute-start.4 = (f32[40,128]{1,0:T(8,128)S(1)}, f32[40,128]{1,0:T(8,128)S(1)}, u32[]{:S(2)}, u32[]{:S(2)}) collective-permute-start(f32[40,128]{1,0:T(8,128)S(1)} %copy-done.4), channel_id=1, source_target_pairs={{0,24},{1,25},{2,26},{3,27},{4,28},{5,29},{6,30},{7,31},{8,16},{9,... | collective-permute-start | bytes 61448 | tf_op jit(solution)/shard_map/ppermute | solution.py:592
  76.4 0.0 collective-permute-start.3
  76.4 22.2 %collective-permute-done.4 = f32[40,128]{1,0:T(8,128)S(1)} collective-permute-done((f32[40,128]{1,0:T(8,128)S(1)}, f32[40,128]{1,0:T(8,128)S(1)}, u32[]{:S(2)}, u32[]{:S(2)}) %collective-permute-start.4) | collective-permute-done | bytes 20512 | tf_op jit(solution)/shard_map/ppermute | solution.py:592
  98.6 0.0 collective-permute-done.3
  98.6 0.0 copy-done.6
  98.6 0.1 collective-permute-start.5
  98.7 1.2 collective-permute-done.5
  100.0 3.5 %collective-permute-start.6 = (f32[8,40,128]{2,1,0:T(8,128)S(1)}, f32[8,40,128]{2,1,0:T(8,128)S(1)}, u32[]{:S(2)}, u32[]{:S(2)}) collective-permute-start(f32[8,40,128]{2,1,0:T(8,128)S(1)} %get-tuple-element.35), channel_id=1, source_target_pairs={{0,2},{1,3},{2,0},{3,1},{4,6},{5,7},{6,4},{7,5},{8,10},{9,11},{10,... | collective-permute-start | bytes 491528 | tf_op jit(solution)/shard_map/ppermute | solution.py:598
  103.5 4.5 %collective-permute-done.6 = f32[8,40,128]{2,1,0:T(8,128)S(1)} collective-permute-done((f32[8,40,128]{2,1,0:T(8,128)S(1)}, f32[8,40,128]{2,1,0:T(8,128)S(1)}, u32[]{:S(2)}, u32[]{:S(2)}) %collective-permute-start.6) | collective-permute-done | bytes 163872 | tf_op jit(solution)/shard_map/ppermute | solution.py:598
  108.0 1.1 collective-permute-start.7
  109.1 0.6 pad_add_fusion.table_ref
  109.7 7.6 %collective-permute-done.7 = f32[16,40,128]{2,1,0:T(8,128)S(1)} collective-permute-done((f32[16,40,128]{2,1,0:T(8,128)S(1)}, f32[16,40,128]{2,1,0:T(8,128)S(1)}, u32[]{:S(2)}, u32[]{:S(2)}) %collective-permute-start.7) | collective-permute-done | bytes 327712 | tf_op jit(solution)/shard_map/ppermute | solution.py:598
  117.3 0.0 copy-start.3
  117.3 0.8 copy-done.3
  118.2 9.9 %forward.1 = (f32[6,32,40,128]{3,2,1,0:T(8,128)}, f32[5,32,8,128]{3,2,1,0:T(8,128)}, f32[5,40,128]{2,1,0:T(8,128)}, f32[32,32,128]{2,1,0:T(8,128)}, f32[32,32,12...) custom-call(f32[32,40,128]{2,1,0:T(8,128)} %copy-done.3), custom_call_target="tpu_custom_call" | custom-call | flops 10000000 | bytes 8000000 | tf_op jit(solution)/shard_map/forward/pallas_call | solution.py:349
  128.0 7.4 %product.2 = (bf16[512,1024]{1,0:T(8,128)(2,1)}, f32[2,1,256]{2,1,0:T(1,128)}) custom-call(s32[2]{0:T(128)} %pad_add_fusion.table_ref, bf16[256,3584]{1,0:T(8,128)(2,1)} %bitcast.42, bf16[1024,3584]{1,0:T(8,128)(2,1)} %bitcast.37, bf16[512,1024]{1,0:T(8,128)(2,1)} %bitcast.43, f32[512,128]{1,0:T(8,128)} %get-tuple-element.17.refs_3_), custom_call_target="tpu_custom_call" | custom-call | flops 1879048192 | bytes 10223616 | tf_op jit(solution)/shard_map/product/pallas_call | solution.py:444
  135.4 0.0 all-to-all-done
  135.4 0.0 copy-start
  135.4 1.3 copy-done
  136.7 7.4 %product.3 = (bf16[512,1024]{1,0:T(8,128)(2,1)}, f32[2,1,256]{2,1,0:T(1,128)}) custom-call(s32[2]{0:T(128)} %pad_add_fusion.table_ref, bf16[256,3584]{1,0:T(8,128)(2,1)} %bitcast.39, bf16[1024,3584]{1,0:T(8,128)(2,1)} %bitcast.38, bf16[512,1024]{1,0:T(8,128)(2,1)} %bitcast.44, ...), custom_call_target="tpu_custom_call", output_to_operand_aliasing={{0}: (5, {}), {1}: (6, {})} | custom-call | flops 1879048192 | bytes 10223616 | tf_op jit(solution)/shard_map/product/pallas_call | solution.py:444
  144.0 0.7 copy.14
  144.7 9.6 %all_to_all.15 = f32[32,2,1,256]{3,1,2,0:T(2,128)S(1)} all-to-all(f32[32,2,1,256]{3,1,2,0:T(2,128)S(1)} %broadcast_in_dim.13), channel_id=1, replica_groups=mesh['half'=2,'plane'=2,'expert'=8] {'half','plane','expert'}, dimensions={0} | all-to-all | bytes 131072 | tf_op jit(solution)/shard_map/all_to_all | solution.py:562
  154.4 0.6 copy.12
  155.0 6.4 %adjoint.1 = (f32[4,128]{1,0:T(4,128)}, f32[32,128]{1,0:T(8,128)}) custom-call(f32[32,512]{1,0:T(8,128)} %bitcast.47, f32[6,32,40,128]{3,2,1,0:T(8,128)} %get-tuple-element.22.level_ref, f32[5,32,8,128]{3,2,1,0:T(8,128)} %get-tuple-element.23.inverse_ref, f32[5,40,128]{2,1,0:T(8,128)} %get-tuple-element.24.column_ref, ...), custom_call_target="tpu_custom_call" | custom-call | flops 10000000 | bytes 8000000 | tf_op jit(solution)/shard_map/adjoint/pallas_call | solution.py:546
  (9 shorter events, 0.1 us)
Async XLA Ops:
  6.2 12.3 %copy-start.4 = (f32[40,128]{1,0:T(8,128)S(1)}, f32[40,128]{1,0:T(8,128)}, u32[]{:S(2)}) copy-start(f32[40,128]{1,0:T(8,128)} %mine.1.small_ref) | copy-start | bytes 61444
  6.2 62.4 %all-to-all-start.1 = ((bf16[16,16,3584]{2,1,0:T(8,128)(2,1)}), bf16[16,16,3584]{2,1,0:T(8,128)(2,1)S(1)}, u32[]{:S(2)}, u32[]{:S(2)}) async-start(bf16[16,16,3584]{2,1,0:T(8,128)(2,1)} %bitcast.41), calls=%async_computation.1 | async-start | bytes 3670016 | tf_op jit(solution)/shard_map/all_to_all | solution.py:608
  12.7 50.5 %collective-permute-start.1 = (bf16[128,3584]{1,0:T(8,128)(2,1)}, bf16[128,3584]{1,0:T(8,128)(2,1)S(1)}, u32[]{:S(2)}, u32[]{:S(2)}) collective-permute-start(bf16[128,3584]{1,0:T(8,128)(2,1)} %refs_0_.1), channel_id=1, source_target_pairs={{0,16},{24,8},{1,17},{25,9},{2,18},{26,10},{3,19},{27,11},{4,20},{... | collective-permute-start | bytes 2752520 | tf_op jit(solution)/shard_map/ppermute | solution.py:603
  17.2 46.0 %collective-permute-start.2 = (bf16[128,3584]{1,0:T(8,128)(2,1)}, bf16[128,3584]{1,0:T(8,128)(2,1)}, u32[]{:S(2)}, u32[]{:S(2)}) collective-permute-start(bf16[128,3584]{1,0:T(8,128)(2,1)} %refs_0_.1), channel_id=1, source_target_pairs={{8,24},{16,0},{9,25},{17,1},{10,26},{18,2},{11,27},{19,3},{12,28},... | collective-permute-start | bytes 2752520 | tf_op jit(solution)/shard_map/ppermute | solution.py:603
  18.5 44.7 %collective-permute-start = (f32[40,128]{1,0:T(8,128)S(1)}, f32[40,128]{1,0:T(8,128)S(1)}, u32[]{:S(2)}, u32[]{:S(2)}) collective-permute-start(f32[40,128]{1,0:T(8,128)S(1)} %copy-done.4), channel_id=1, source_target_pairs={{0,16},{1,17},{2,18},{3,19},{4,20},{5,21},{6,22},{7,23},{8,24},{9,... | collective-permute-start | bytes 61448 | tf_op jit(solution)/shard_map/ppermute | solution.py:592
  63.2 0.6 copy-start.5
  63.2 0.9 copy-start.2
  68.6 1.2 copy-start.1
  68.6 30.0 %copy-start.6 = (f32[40,128]{1,0:T(8,128)S(1)}, f32[40,128]{1,0:T(8,128)}, u32[]{:S(2)}) copy-start(f32[40,128]{1,0:T(8,128)} %copy-done.5) | copy-start | bytes 61444
  69.9 65.5 %all-to-all-start = ((bf16[16,16,3584]{2,1,0:T(8,128)(2,1)}), bf16[16,16,3584]{2,1,0:T(8,128)(2,1)S(1)}, u32[]{:S(2)}, u32[]{:S(2)}) async-start(bf16[16,16,3584]{2,1,0:T(8,128)(2,1)} %bitcast.40), calls=%async_computation | async-start | bytes 3670016 | tf_op jit(solution)/shard_map/all_to_all | solution.py:608
  73.8 24.8 %collective-permute-start.4 = (f32[40,128]{1,0:T(8,128)S(1)}, f32[40,128]{1,0:T(8,128)S(1)}, u32[]{:S(2)}, u32[]{:S(2)}) collective-permute-start(f32[40,128]{1,0:T(8,128)S(1)} %copy-done.4), channel_id=1, source_target_pairs={{0,24},{1,25},{2,26},{3,27},{4,28},{5,29},{6,30},{7,31},{8,16},{9,... | collective-permute-start | bytes 61448 | tf_op jit(solution)/shard_map/ppermute | solution.py:592
  76.4 22.2 %collective-permute-start.3 = (f32[40,128]{1,0:T(8,128)S(1)}, f32[40,128]{1,0:T(8,128)S(1)}, u32[]{:S(2)}, u32[]{:S(2)}) collective-permute-start(f32[40,128]{1,0:T(8,128)S(1)} %copy-done.4), channel_id=1, source_target_pairs={{0,8},{1,9},{2,10},{3,11},{4,12},{5,13},{6,14},{7,15},{8,0},{9,1},... | collective-permute-start | bytes 61448 | tf_op jit(solution)/shard_map/ppermute | solution.py:592
  98.6 1.3 collective-permute-start.5
  100.0 8.0 %collective-permute-start.6 = (f32[8,40,128]{2,1,0:T(8,128)S(1)}, f32[8,40,128]{2,1,0:T(8,128)S(1)}, u32[]{:S(2)}, u32[]{:S(2)}) collective-permute-start(f32[8,40,128]{2,1,0:T(8,128)S(1)} %get-tuple-element.35), channel_id=1, source_target_pairs={{0,2},{1,3},{2,0},{3,1},{4,6},{5,7},{6,4},{7,5},{8,10},{9,11},{10,... | collective-permute-start | bytes 491528 | tf_op jit(solution)/shard_map/ppermute | solution.py:598
  108.0 9.3 %collective-permute-start.7 = (f32[16,40,128]{2,1,0:T(8,128)S(1)}, f32[16,40,128]{2,1,0:T(8,128)S(1)}, u32[]{:S(2)}, u32[]{:S(2)}) collective-permute-start(f32[16,40,128]{2,1,0:T(8,128)S(1)} %get-tuple-element.31), channel_id=1, source_target_pairs={{0,4},{1,5},{2,6},{3,7},{4,0},{5,1},{6,2},{7,3},{8,12},{9,13},{10,... | collective-permute-start | bytes 983048 | tf_op jit(solution)/shard_map/ppermute | solution.py:598
  117.3 0.8 copy-start.3
  135.4 1.3 copy-start

commit v4 on v3

--- a/solution.py
+++ b/solution.py
@@ -15,6 +15,7 @@
 AXES = ("half", "plane", "expert")
 NEAR = ("plane", "expert")
 REPLICATED_BYTES = 1 << 20
+PRODUCT_VMEM = 58880 << 10
 
 
 def capped(logits):
@@ -367,23 +368,14 @@
     )(everyone)
 
 
-def product_kernel(table_ref, *refs, carried, last, extra):
-    refs = list(refs)
-    rows_ref, weight_ref = refs[:2]
-    del refs[:2]
+def product_kernel(table_ref, rows_ref, weight_ref, saved_ref, gate_ref, *refs):
+    grad_ref, slot_ref, sum_ref = refs[-3:]
     unscaled = lax.dot_general(
         rows_ref[...],
         weight_ref[...],
         (((1,), (1,)), ((), ())),
         preferred_element_type=jnp.float32,
     )
-    if carried:
-        unscaled = unscaled + refs.pop(0)[...]
-    if not last:
-        refs[extra][...] = unscaled
-        return
-    saved_ref, gate_ref = refs[:2]
-    grad_ref, slot_ref, sum_ref = refs[-3:]
     grad_ref[...] = (gate_ref[:, :1] * unscaled).astype(grad_ref.dtype)
     partial_sums = unscaled * saved_ref[...].astype(jnp.float32)
     folded = partial_sums[:, :LANES]
@@ -401,69 +393,53 @@
 
     @pl.when(pl.program_id(0) == pl.num_programs(0) - 1)
     def _():
-        slot_ref[0] = jnp.sum(sum_ref[...].T, 0, keepdims=True)
-
-
-def product(
-    table, entry, rows, weight, saved, gates, part=0, carried=None, last=True, earlier=None, after=()
-):
+        sums = jnp.sum(sum_ref[...].T, 0, keepdims=True)
+        for d in range(slot_ref.shape[0]):
+            slot_ref[d, 0] = sums
+
+
+def product(table, entry, rows, weight, saved, gates, copies, earlier=()):
     slots, width = rows.shape
     hidden = weight.shape[0]
     total = saved.shape[0]
-    block = 256 if hidden % 256 == 0 else hidden
+    block = 512 if hidden % 512 == 0 else hidden
     row_block = pl.BlockSpec((slots, block), lambda i, table: (table[entry], i))
-    own_block = pl.BlockSpec((slots, block), lambda i, table: (0, i))
-    operands = [rows, weight]
-    in_specs = [
-        pl.BlockSpec((slots, width), lambda i, table: (0, 0)),
-        pl.BlockSpec((block, width), lambda i, table: (i, part)),
-    ]
-    aliases = {}
-    if carried is not None:
-        operands.append(carried)
-        in_specs.append(own_block)
-    if last:
-        operands += [saved, gates]
-        in_specs += [row_block, pl.BlockSpec((slots, LANES), lambda i, table: (table[entry], 0))]
-        if earlier is not None:
-            aliases = {len(operands) + 1 + i: i for i in range(2)}
-            operands += earlier
-            in_specs += [pl.BlockSpec(memory_space=pl.ANY)] * 2
-        out_shape = [
+    return pl.pallas_call(
+        product_kernel,
+        out_shape=[
             jax.ShapeDtypeStruct((total, hidden), jnp.bfloat16),
-            jax.ShapeDtypeStruct((total // slots, 1, slots), jnp.float32),
-        ]
-        out_specs = [row_block, pl.BlockSpec((1, 1, slots), lambda i, table: (table[entry], 0, 0))]
-        scratch = [pltpu.VMEM((slots, LANES), jnp.float32)]
-    else:
-        out_shape = jax.ShapeDtypeStruct((slots, hidden), jnp.float32)
-        out_specs = own_block
-        scratch = []
-    operands += after
-    in_specs += [pl.BlockSpec(memory_space=pl.ANY)] * len(after)
-    return pl.pallas_call(
-        partial(product_kernel, carried=carried is not None, last=last, extra=len(after)),
-        out_shape=out_shape,
+            jax.ShapeDtypeStruct((copies, total // slots, 1, slots), jnp.float32),
+        ],
         grid_spec=pltpu.PrefetchScalarGridSpec(
             num_scalar_prefetch=1,
             grid=(hidden // block,),
-            in_specs=in_specs,
-            out_specs=out_specs,
-            scratch_shapes=scratch,
+            in_specs=[
+                pl.BlockSpec((slots, width), lambda i, table: (0, 0)),
+                pl.BlockSpec((block, width), lambda i, table: (i, 0)),
+                row_block,
+                pl.BlockSpec((slots, LANES), lambda i, table: (table[entry], 0)),
+            ]
+            + [pl.BlockSpec(memory_space=pl.ANY)] * len(earlier),
+            out_specs=[
+                row_block,
+                pl.BlockSpec((copies, 1, 1, slots), lambda i, table: (0, table[entry], 0, 0)),
+            ],
+            scratch_shapes=[pltpu.VMEM((slots, LANES), jnp.float32)],
         ),
-        input_output_aliases=aliases,
+        input_output_aliases={5 + i: i for i in range(len(earlier))},
+        compiler_params=pltpu.CompilerParams(vmem_limit_bytes=PRODUCT_VMEM),
         cost_estimate=pl.CostEstimate(
             flops=2 * slots * width * hidden,
             bytes_accessed=2 * (slots * width + hidden * width + 2 * slots * hidden),
             transcendentals=0,
         ),
         name="product",
-    )(table, *operands)
+    )(table, rows, weight, saved, gates, *earlier)
 
 
 def adjoint_kernel(
-    slot_ref, level_ref, inverse_ref, column_ref, seed_q_ref, seed_p_ref, where_ref,
-    own_ref, group_ref, expert_ref, carry_ref, *, groups, capacity, targets
+    answer_ref, level_ref, inverse_ref, column_ref, seed_q_ref, seed_p_ref, where_ref,
+    own_ref, group_ref, expert_ref, carry_ref, slot_ref, *, groups, capacity, targets
 ):
     devices = level_ref.shape[1]
     tiles = groups + 1
@@ -471,6 +447,10 @@
     row_id = lax.broadcasted_iota(jnp.int32, tile, 0)
     zero = jnp.zeros(tile, jnp.float32)
     per_block = LANES // capacity
+    width = answer_ref.shape[3]
+    for e in range(answer_ref.shape[0]):
+        for h in range(answer_ref.shape[1]):
+            slot_ref[e : e + 1, h * width : (h + 1) * width] = answer_ref[e, h]
 
     def seeds(d):
         block = pl.ds(pl.multiple_of(lax.div(d, per_block) * LANES, LANES), LANES)
@@ -551,15 +531,14 @@
         ],
         in_specs=[vmem] * (2 + len(saved)),
         out_specs=[vmem, vmem],
-        scratch_shapes=[pltpu.VMEM(level.shape[1:], jnp.float32)],
+        scratch_shapes=[
+            pltpu.VMEM(level.shape[1:], jnp.float32),
+            pltpu.VMEM((groups * SUBLANES, level.shape[1] * capacity), jnp.float32),
+        ],
+        compiler_params=pltpu.CompilerParams(vmem_limit_bytes=24 << 20),
         cost_estimate=pl.CostEstimate(flops=10_000_000, bytes_accessed=8_000_000, transcendentals=0),
         name="adjoint",
     )(slot_grads, *saved, own)
-
-
-def spread(block, axes):
-    copies = jnp.broadcast_to(block[None], (lax.axis_size(axes),) + block.shape)
-    return lax.all_to_all(copies, axes, split_axis=0, concat_axis=0)
 
 
 def cube_bits(groups, per_group):
@@ -612,10 +591,10 @@
     own_rows = send(mine, [cotangent])
     other_rows = send(other, swapped)
     *saved, gates, own = forward(everyone, cube, groups, top_count, capacity, targets)
-    result = product(table, 0, own_rows, weight, hidden, gates)
-    result = product(table, 1, other_rows, weight, hidden, gates, earlier=list(result))
+    result = product(table, 0, own_rows, weight, hidden, gates, experts)
+    result = product(table, 1, other_rows, weight, hidden, gates, experts, result)
     hidden_grad, slot_grad = result
-    slot_grads = spread(slot_grad, AXES).reshape(experts, -1)
+    slot_grads = lax.all_to_all(slot_grad, AXES, split_axis=0, concat_axis=0)
     d_group, d_expert = adjoint(slot_grads, saved, own, groups, capacity, targets)
     return (hidden_grad[None], d_group.T, d_expert.T)
 

time: 162 us -> 156 us (0.963)
  Pallas kernels: 41.1 us -> 37.2 us
  local copies, waits for them, and re-layouts: 5.66 us -> 3.2 us
    pallas_call x1, Pallas kernels: 6.4 us -> 3.64 us  [adjoint(): pl.pallas_call(partial(adjoint_kernel, groups=groups, capacity=capacity,...]
    unnamed x21 -> x31, local copies, waits for them, and re-layouts: 5.6 us -> 3.16 us
where the time goes in v4:
time: 156 us
  waiting for transfers between devices  75.7 us (49%)
  Pallas kernels  37.2 us (24%)
  starting transfers between devices  27.9 us (18%)
  blocking collectives  10.2 us (7%)
  local copies, waits for them, and re-layouts  3.2 us (2%)
    ppermute x3, waiting for transfers between devices, replicated(): column.append(lax.ppermute(mine, AXES, pairs))  62.4 us
    pallas_call x2, Pallas kernels, product(): pl.pallas_call(product_kernel, out_shape=[jax.ShapeDtypeStruct((total, hi...  13.7 us
    ppermute x3, waiting for transfers between devices, replicated(): everyone = jnp.concatenate([everyone, lax.ppermute(everyone, AXES, pairs)])  13.3 us
    all_to_all x2, starting transfers between devices, send(): got = lax.all_to_all(packed, NEAR, split_axis=0, concat_axis=0)  10.9 us
    all_to_all x1, blocking collectives, replicated(): slot_grads = lax.all_to_all(slot_grad, AXES, split_axis=0, concat_axis=0)  10.2 us
    pallas_call x1, Pallas kernels, forward(): pl.pallas_call(partial(forward_kernel, groups=groups, top_count=top_count...  9.69 us
    pallas_call x2, Pallas kernels, pack_rows(): pl.pallas_call(partial(pack_kernel, near=near, capacity=capacity, first_i...  8.74 us
    ppermute x3, starting transfers between devices, replicated(): column.append(lax.ppermute(mine, AXES, pairs))  6.57 us
  transfers between devices with their start and end apart: 10, of which 5 were waited for; matrix products, arithmetic and copies ran while one was open for 0% of the time, Pallas kernels for 13%

profile of v4, /device:TPU:0, one launch (start us, length us, event | category | flops | bytes accessed | tf_op | source)
XLA Modules:
  0.0 155.6 jit_solution(67893651059218719)
XLA Ops:
  0.6 1.4 mine.1.small_ref
  2.0 4.2 %pack_rows.3 = bf16[256,3584]{1,0:T(8,128)(2,1)} custom-call(f32[40,128]{1,0:T(8,128)} %mine.1.small_ref, bf16[128,3584]{1,0:T(8,128)(2,1)} %refs_0_.1), custom_call_target="tpu_custom_call" | custom-call | flops 234881024 | bytes 2752512 | tf_op jit(solution)/shard_map/pack_rows/pallas_call | solution.py:190
  6.2 0.0 copy-start.10
  6.2 6.4 %all-to-all-start.1 = ((bf16[16,16,3584]{2,1,0:T(8,128)(2,1)}), bf16[16,16,3584]{2,1,0:T(8,128)(2,1)S(1)}, u32[]{:S(2)}, u32[]{:S(2)}) async-start(bf16[16,16,3584]{2,1,0:T(8,128)(2,1)} %bitcast.33), calls=%async_computation.1 | async-start | bytes 3670016 | tf_op jit(solution)/shard_map/all_to_all | solution.py:587
  12.7 4.6 %collective-permute-start.1 = (bf16[128,3584]{1,0:T(8,128)(2,1)}, bf16[128,3584]{1,0:T(8,128)(2,1)S(1)}, u32[]{:S(2)}, u32[]{:S(2)}) collective-permute-start(bf16[128,3584]{1,0:T(8,128)(2,1)} %refs_0_.1), channel_id=1, source_target_pairs={{0,16},{24,8},{1,17},{25,9},{2,18},{26,10},{3,19},{27,11},{4,20},{... | collective-permute-start | bytes 2752520 | tf_op jit(solution)/shard_map/ppermute | solution.py:582
  17.2 1.3 collective-permute-start.2
  18.5 0.0 copy-done.10
  18.5 4.5 %collective-permute-start = (f32[40,128]{1,0:T(8,128)S(1)}, f32[40,128]{1,0:T(8,128)S(1)}, u32[]{:S(2)}, u32[]{:S(2)}) collective-permute-start(f32[40,128]{1,0:T(8,128)S(1)} %copy-done.10), channel_id=1, source_target_pairs={{0,16},{1,17},{2,18},{3,19},{4,20},{5,21},{6,22},{7,23},{8,24},{9,... | collective-permute-start | bytes 61448 | tf_op jit(solution)/shard_map/ppermute | solution.py:571
  23.0 40.2 %collective-permute-done.small_ref = f32[40,128]{1,0:T(8,128)S(1)} collective-permute-done((f32[40,128]{1,0:T(8,128)S(1)}, f32[40,128]{1,0:T(8,128)S(1)}, u32[]{:S(2)}, u32[]{:S(2)}) %collective-permute-start) | collective-permute-done | bytes 20512 | tf_op jit(solution)/shard_map/ppermute | solution.py:571
  63.2 0.0 copy-start.11
  63.2 0.0 collective-permute-done.1.refs_0_
  63.2 0.0 copy-start.8
  63.2 0.0 collective-permute-done.2.refs_1_
  63.2 0.6 copy-done.11
  63.8 0.3 copy-done.8
  64.1 4.5 %pack_rows.2 = bf16[256,3584]{1,0:T(8,128)(2,1)} custom-call(f32[40,128]{1,0:T(8,128)} %copy-done.11, bf16[128,3584]{1,0:T(8,128)(2,1)} %copy-done.8, bf16[128,3584]{1,0:T(8,128)(2,1)} %collective-permute-done.2.refs_1_), custom_call_target="tpu_custom_call" | custom-call | flops 234881024 | bytes 2752512 | tf_op jit(solution)/shard_map/pack_rows/pallas_call | solution.py:190
  68.6 0.0 all-to-all-done.1
  68.7 0.0 copy-start.7
  68.7 0.0 copy-start.12
  68.7 1.3 copy-done.7
  70.0 4.4 %all-to-all-start = ((bf16[16,16,3584]{2,1,0:T(8,128)(2,1)}), bf16[16,16,3584]{2,1,0:T(8,128)(2,1)}, u32[]{:S(2)}, u32[]{:S(2)}) async-start(bf16[16,16,3584]{2,1,0:T(8,128)(2,1)} %bitcast.32), calls=%async_computation | async-start | bytes 3670016 | tf_op jit(solution)/shard_map/all_to_all | solution.py:587
  74.4 2.1 %collective-permute-start.4 = (f32[40,128]{1,0:T(8,128)S(1)}, f32[40,128]{1,0:T(8,128)S(1)}, u32[]{:S(2)}, u32[]{:S(2)}) collective-permute-start(f32[40,128]{1,0:T(8,128)S(1)} %copy-done.10), channel_id=1, source_target_pairs={{0,24},{1,25},{2,26},{3,27},{4,28},{5,29},{6,30},{7,31},{8,16},{9,... | collective-permute-start | bytes 61448 | tf_op jit(solution)/shard_map/ppermute | solution.py:571
  76.5 0.0 collective-permute-start.3
  76.5 22.2 %collective-permute-done.4 = f32[40,128]{1,0:T(8,128)S(1)} collective-permute-done((f32[40,128]{1,0:T(8,128)S(1)}, f32[40,128]{1,0:T(8,128)S(1)}, u32[]{:S(2)}, u32[]{:S(2)}) %collective-permute-start.4) | collective-permute-done | bytes 20512 | tf_op jit(solution)/shard_map/ppermute | solution.py:571
  98.7 0.0 collective-permute-done.3
  98.7 0.0 copy-done.12
  98.8 0.1 collective-permute-start.5
  98.9 1.2 collective-permute-done.5
  100.1 3.5 %collective-permute-start.6 = (f32[8,40,128]{2,1,0:T(8,128)S(1)}, f32[8,40,128]{2,1,0:T(8,128)S(1)}, u32[]{:S(2)}, u32[]{:S(2)}) collective-permute-start(f32[8,40,128]{2,1,0:T(8,128)S(1)} %get-tuple-element.35), channel_id=1, source_target_pairs={{0,2},{1,3},{2,0},{3,1},{4,6},{5,7},{6,4},{7,5},{8,10},{9,11},{10,... | collective-permute-start | bytes 491528 | tf_op jit(solution)/shard_map/ppermute | solution.py:577
  103.6 4.5 %collective-permute-done.6 = f32[8,40,128]{2,1,0:T(8,128)S(1)} collective-permute-done((f32[8,40,128]{2,1,0:T(8,128)S(1)}, f32[8,40,128]{2,1,0:T(8,128)S(1)}, u32[]{:S(2)}, u32[]{:S(2)}) %collective-permute-start.6) | collective-permute-done | bytes 163872 | tf_op jit(solution)/shard_map/ppermute | solution.py:577
  108.2 1.1 collective-permute-start.7
  109.2 0.6 pad_add_fusion.table_ref
  109.8 7.6 %collective-permute-done.7 = f32[16,40,128]{2,1,0:T(8,128)S(1)} collective-permute-done((f32[16,40,128]{2,1,0:T(8,128)S(1)}, f32[16,40,128]{2,1,0:T(8,128)S(1)}, u32[]{:S(2)}, u32[]{:S(2)}) %collective-permute-start.7) | collective-permute-done | bytes 327712 | tf_op jit(solution)/shard_map/ppermute | solution.py:577
  117.5 0.0 copy-start.9
  117.5 0.8 copy-done.9
  118.3 9.7 %forward.1 = (f32[6,32,40,128]{3,2,1,0:T(8,128)}, f32[5,32,8,128]{3,2,1,0:T(8,128)}, f32[5,40,128]{2,1,0:T(8,128)}, f32[32,32,128]{2,1,0:T(8,128)}, f32[32,32,12...) custom-call(f32[32,40,128]{2,1,0:T(8,128)} %copy-done.9), custom_call_target="tpu_custom_call" | custom-call | flops 10000000 | bytes 8000000 | tf_op jit(solution)/shard_map/forward/pallas_call | solution.py:350
  128.0 6.6 %product.2 = (bf16[512,1024]{1,0:T(8,128)(2,1)}, f32[32,2,1,256]{3,2,1,0:T(1,128)}) custom-call(s32[2]{0:T(128)} %pad_add_fusion.table_ref, bf16[256,3584]{1,0:T(8,128)(2,1)} %bitcast.34, bf16[1024,3584]{1,0:T(8,128)(2,1)} %bitcast.30, bf16[512,1024]{1,0:T(8,128)(2,1)} %bitcast.35, f32[512,128]{1,0:T(8,128)} %get-tuple-element.17.gate_ref), custom_call_target="tpu_custom_call" | custom-call | flops 1879048192 | bytes 10223616 | tf_op jit(solution)/shard_map/product/pallas_call | solution.py:407
  134.6 0.0 all-to-all-done
  134.6 0.0 copy-start
  134.6 0.0 copy-start.1
  134.6 0.0 copy-start.2
  134.6 0.0 copy-start.3
  134.6 0.0 copy-start.4
  134.6 0.0 copy-start.5
  134.6 0.0 copy-start.6
  134.6 7.1 %product.3 = (bf16[512,1024]{1,0:T(8,128)(2,1)}, f32[32,2,1,256]{3,2,1,0:T(1,128)}) custom-call(s32[2]{0:T(128)} %pad_add_fusion.table_ref, bf16[256,3584]{1,0:T(8,128)(2,1)} %bitcast.6.rows_ref, bf16[1024,3584]{1,0:T(8,128)(2,1)} %bitcast.31, bf16[512,1024]{1,0:T(8,128)(2,1)} %bitcast.36, ...), custom_call_target="tpu_custom_call", output_to_operand_aliasing={{0}: (5, {}), {1}: (6, {})} | custom-call | flops 1879048192 | bytes 10223616 | tf_op jit(solution)/shard_map/product/pallas_call | solution.py:407
  141.8 10.2 %all_to_all.15.answer_ref = f32[32,2,1,256]{3,2,1,0:T(1,128)S(1)} all-to-all(f32[32,2,1,256]{3,2,1,0:T(1,128)} %get-tuple-element.21), channel_id=1, replica_groups=mesh['half'=2,'plane'=2,'expert'=8] {'half','plane','expert'}, dimensions={0} | all-to-all | bytes 131072 | tf_op jit(solution)/shard_map/all_to_all | solution.py:597
  151.9 0.0 copy-done
  151.9 0.0 copy-done.1
  151.9 0.0 copy-done.2
  152.0 0.0 copy-done.3
  152.0 0.0 copy-done.4
  152.0 0.0 copy-done.5
  152.0 0.0 copy-done.6
  152.0 3.6 %adjoint.1 = (f32[4,128]{1,0:T(4,128)}, f32[32,128]{1,0:T(8,128)}) custom-call(f32[32,2,1,256]{3,2,1,0:T(1,128)S(1)} %all_to_all.15.answer_ref, f32[6,32,40,128]{3,2,1,0:T(8,128)S(1)} %copy-done, f32[5,32,8,128]{3,2,1,0:T(8,128)S(1)} %copy-done.1, f32[5,40,128]{2,1,0:T(8,128)S(1)} %copy-done.5, f32[32,32,128]{2,1,0:T(8,128)S(1)} %copy-done.2, ...), custom_call_target="tpu_custom_call" | custom-call | flops 10000000 | bytes 8000000 | tf_op jit(solution)/shard_map/adjoint/pallas_call | solution.py:526
  (8 shorter events, 0.1 us)
Async XLA Ops:
  6.2 12.3 %copy-start.10 = (f32[40,128]{1,0:T(8,128)S(1)}, f32[40,128]{1,0:T(8,128)}, u32[]{:S(2)}) copy-start(f32[40,128]{1,0:T(8,128)} %mine.1.small_ref) | copy-start | bytes 61444
  6.2 62.4 %all-to-all-start.1 = ((bf16[16,16,3584]{2,1,0:T(8,128)(2,1)}), bf16[16,16,3584]{2,1,0:T(8,128)(2,1)S(1)}, u32[]{:S(2)}, u32[]{:S(2)}) async-start(bf16[16,16,3584]{2,1,0:T(8,128)(2,1)} %bitcast.33), calls=%async_computation.1 | async-start | bytes 3670016 | tf_op jit(solution)/shard_map/all_to_all | solution.py:587
  12.7 50.5 %collective-permute-start.1 = (bf16[128,3584]{1,0:T(8,128)(2,1)}, bf16[128,3584]{1,0:T(8,128)(2,1)S(1)}, u32[]{:S(2)}, u32[]{:S(2)}) collective-permute-start(bf16[128,3584]{1,0:T(8,128)(2,1)} %refs_0_.1), channel_id=1, source_target_pairs={{0,16},{24,8},{1,17},{25,9},{2,18},{26,10},{3,19},{27,11},{4,20},{... | collective-permute-start | bytes 2752520 | tf_op jit(solution)/shard_map/ppermute | solution.py:582
  17.2 46.0 %collective-permute-start.2 = (bf16[128,3584]{1,0:T(8,128)(2,1)}, bf16[128,3584]{1,0:T(8,128)(2,1)}, u32[]{:S(2)}, u32[]{:S(2)}) collective-permute-start(bf16[128,3584]{1,0:T(8,128)(2,1)} %refs_0_.1), channel_id=1, source_target_pairs={{8,24},{16,0},{9,25},{17,1},{10,26},{18,2},{11,27},{19,3},{12,28},... | collective-permute-start | bytes 2752520 | tf_op jit(solution)/shard_map/ppermute | solution.py:582
  18.5 44.7 %collective-permute-start = (f32[40,128]{1,0:T(8,128)S(1)}, f32[40,128]{1,0:T(8,128)S(1)}, u32[]{:S(2)}, u32[]{:S(2)}) collective-permute-start(f32[40,128]{1,0:T(8,128)S(1)} %copy-done.10), channel_id=1, source_target_pairs={{0,16},{1,17},{2,18},{3,19},{4,20},{5,21},{6,22},{7,23},{8,24},{9,... | collective-permute-start | bytes 61448 | tf_op jit(solution)/shard_map/ppermute | solution.py:571
  63.2 0.6 copy-start.11
  63.2 0.9 copy-start.8
  68.7 1.3 copy-start.7
  68.7 30.1 %copy-start.12 = (f32[40,128]{1,0:T(8,128)S(1)}, f32[40,128]{1,0:T(8,128)}, u32[]{:S(2)}) copy-start(f32[40,128]{1,0:T(8,128)} %copy-done.11) | copy-start | bytes 61444
  70.0 64.6 %all-to-all-start = ((bf16[16,16,3584]{2,1,0:T(8,128)(2,1)}), bf16[16,16,3584]{2,1,0:T(8,128)(2,1)}, u32[]{:S(2)}, u32[]{:S(2)}) async-start(bf16[16,16,3584]{2,1,0:T(8,128)(2,1)} %bitcast.32), calls=%async_computation | async-start | bytes 3670016 | tf_op jit(solution)/shard_map/all_to_all | solution.py:587
  74.4 24.3 %collective-permute-start.4 = (f32[40,128]{1,0:T(8,128)S(1)}, f32[40,128]{1,0:T(8,128)S(1)}, u32[]{:S(2)}, u32[]{:S(2)}) collective-permute-start(f32[40,128]{1,0:T(8,128)S(1)} %copy-done.10), channel_id=1, source_target_pairs={{0,24},{1,25},{2,26},{3,27},{4,28},{5,29},{6,30},{7,31},{8,16},{9,... | collective-permute-start | bytes 61448 | tf_op jit(solution)/shard_map/ppermute | solution.py:571
  76.5 22.2 %collective-permute-start.3 = (f32[40,128]{1,0:T(8,128)S(1)}, f32[40,128]{1,0:T(8,128)S(1)}, u32[]{:S(2)}, u32[]{:S(2)}) collective-permute-start(f32[40,128]{1,0:T(8,128)S(1)} %copy-done.10), channel_id=1, source_target_pairs={{0,8},{1,9},{2,10},{3,11},{4,12},{5,13},{6,14},{7,15},{8,0},{9,1},... | collective-permute-start | bytes 61448 | tf_op jit(solution)/shard_map/ppermute | solution.py:571
  98.8 1.3 collective-permute-start.5
  100.1 8.0 %collective-permute-start.6 = (f32[8,40,128]{2,1,0:T(8,128)S(1)}, f32[8,40,128]{2,1,0:T(8,128)S(1)}, u32[]{:S(2)}, u32[]{:S(2)}) collective-permute-start(f32[8,40,128]{2,1,0:T(8,128)S(1)} %get-tuple-element.35), channel_id=1, source_target_pairs={{0,2},{1,3},{2,0},{3,1},{4,6},{5,7},{6,4},{7,5},{8,10},{9,11},{10,... | collective-permute-start | bytes 491528 | tf_op jit(solution)/shard_map/ppermute | solution.py:577
  108.2 9.3 %collective-permute-start.7 = (f32[16,40,128]{2,1,0:T(8,128)S(1)}, f32[16,40,128]{2,1,0:T(8,128)S(1)}, u32[]{:S(2)}, u32[]{:S(2)}) collective-permute-start(f32[16,40,128]{2,1,0:T(8,128)S(1)} %get-tuple-element.31), channel_id=1, source_target_pairs={{0,4},{1,5},{2,6},{3,7},{4,0},{5,1},{6,2},{7,3},{8,12},{9,13},{10,... | collective-permute-start | bytes 983048 | tf_op jit(solution)/shard_map/ppermute | solution.py:577
  117.5 0.8 copy-start.9
  134.6 17.4 %copy-start = (f32[6,32,40,128]{3,2,1,0:T(8,128)S(1)}, f32[6,32,40,128]{3,2,1,0:T(8,128)}, u32[]{:S(2)}) copy-start(f32[6,32,40,128]{3,2,1,0:T(8,128)} %get-tuple-element.22.level_ref) | copy-start | bytes 11796484
  134.6 17.4 %copy-start.1 = (f32[5,32,8,128]{3,2,1,0:T(8,128)S(1)}, f32[5,32,8,128]{3,2,1,0:T(8,128)}, u32[]{:S(2)}) copy-start(f32[5,32,8,128]{3,2,1,0:T(8,128)} %get-tuple-element.23.inverse_ref) | copy-start | bytes 1966084
  134.6 17.4 %copy-start.2 = (f32[32,32,128]{2,1,0:T(8,128)S(1)}, f32[32,32,128]{2,1,0:T(8,128)}, u32[]{:S(2)}) copy-start(f32[32,32,128]{2,1,0:T(8,128)} %get-tuple-element.25.seed_q_ref) | copy-start | bytes 1572868
  134.6 17.4 %copy-start.3 = (f32[32,32,128]{2,1,0:T(8,128)S(1)}, f32[32,32,128]{2,1,0:T(8,128)}, u32[]{:S(2)}) copy-start(f32[32,32,128]{2,1,0:T(8,128)} %get-tuple-element.26.seed_p_ref) | copy-start | bytes 1572868
  134.6 17.4 %copy-start.4 = (s32[32,32,128]{2,1,0:T(8,128)S(1)}, s32[32,32,128]{2,1,0:T(8,128)}, u32[]{:S(2)}) copy-start(s32[32,32,128]{2,1,0:T(8,128)} %get-tuple-element.27.where_ref) | copy-start | bytes 1572868
  134.6 17.4 %copy-start.5 = (f32[5,40,128]{2,1,0:T(8,128)S(1)}, f32[5,40,128]{2,1,0:T(8,128)}, u32[]{:S(2)}) copy-start(f32[5,40,128]{2,1,0:T(8,128)} %get-tuple-element.24.column_ref) | copy-start | bytes 307204
  134.6 17.4 %copy-start.6 = (f32[40,128]{1,0:T(8,128)S(1)}, f32[40,128]{1,0:T(8,128)}, u32[]{:S(2)}) copy-start(f32[40,128]{1,0:T(8,128)} %get-tuple-element.28.own_ref) | copy-start | bytes 61444

commit v5 on v4

--- a/solution.py
+++ b/solution.py
@@ -15,7 +15,8 @@
 AXES = ("half", "plane", "expert")
 NEAR = ("plane", "expert")
 REPLICATED_BYTES = 1 << 20
-PRODUCT_VMEM = 58880 << 10
+OWN_VMEM = 24 << 20
+OTHER_VMEM = 58880 << 10
 
 
 def capped(logits):
@@ -163,40 +164,67 @@
     out_ref[SUBLANES:, :] = expert_ref[...]
 
 
-def pack_kernel(small_ref, *refs, near, capacity, first_id, top_count):
-    *rows_refs, out_ref, place_ref = refs
-
-    @pl.when(pl.program_id(0) == 0)
-    def _():
-        ids = [
-            small_ref[first_id + k : first_id + k + 1, :].astype(jnp.int32)
-            for k in range(top_count)
-        ]
-        place_ref[...] = place_rows(ids, lax.axis_index("half") * near, near, capacity)
-
-    rows = rows_refs[0][...]
-    for rows_ref in rows_refs[1:]:
-        rows = rows + rows_ref[...]
-    out_ref[...] = jnp.dot(
-        place_ref[...], rows, preferred_element_type=jnp.float32
-    ).astype(out_ref.dtype)
+def pack_kernel(small_ref, *refs, near, capacity, first_id, top_count, pieces):
+    *sources, out_ref, rows_ref, packed_ref, in_sem, out_sem = refs
+    width = out_ref.shape[1] // pieces
+    incoming, outgoing = [], []
+    for c in range(pieces):
+        at = pl.ds(c * width, width)
+        incoming.append(
+            [
+                pltpu.make_async_copy(source.at[:, at], rows_ref.at[s, :, at], in_sem.at[s, c])
+                for s, source in enumerate(sources)
+            ]
+        )
+        outgoing.append(
+            pltpu.make_async_copy(packed_ref.at[:, at], out_ref.at[:, at], out_sem.at[c])
+        )
+    for copies in incoming:
+        for copy in copies:
+            copy.start()
+    ids = [
+        small_ref[first_id + k : first_id + k + 1, :].astype(jnp.int32) for k in range(top_count)
+    ]
+    place = place_rows(ids, lax.axis_index("half") * near, near, capacity)
+    for c in range(pieces):
+        at = pl.ds(c * width, width)
+        for copy in incoming[c]:
+            copy.wait()
+        rows = rows_ref[0, :, at]
+        for s in range(1, len(sources)):
+            rows = rows + rows_ref[s, :, at]
+        packed_ref[:, at] = jnp.dot(place, rows, preferred_element_type=jnp.float32).astype(
+            packed_ref.dtype
+        )
+        outgoing[c].start()
+    for copy in outgoing:
+        copy.wait()
 
 
 def pack_rows(small, rows, near, capacity, first_id, top_count):
     tokens, width = rows[0].shape
     dtype = rows[0].dtype
     slots = near * capacity
-    block = max(n for n in range(LANES, 8 * LANES, LANES) if width % n == 0)
+    pieces = max(n for n in range(1, SUBLANES) if width % (n * LANES) == 0)
+    anywhere = pl.BlockSpec(memory_space=pl.ANY)
     return pl.pallas_call(
         partial(
-            pack_kernel, near=near, capacity=capacity, first_id=first_id, top_count=top_count
+            pack_kernel,
+            near=near,
+            capacity=capacity,
+            first_id=first_id,
+            top_count=top_count,
+            pieces=pieces,
         ),
         out_shape=jax.ShapeDtypeStruct((slots, width), dtype),
-        grid=(width // block,),
-        in_specs=[pl.BlockSpec(small.shape, lambda i: (0, 0))]
-        + [pl.BlockSpec((tokens, block), lambda i: (0, i))] * len(rows),
-        out_specs=pl.BlockSpec((slots, block), lambda i: (0, i)),
-        scratch_shapes=[pltpu.VMEM((slots, tokens), dtype)],
+        in_specs=[pl.BlockSpec(memory_space=pltpu.VMEM)] + [anywhere] * len(rows),
+        out_specs=anywhere,
+        scratch_shapes=[
+            pltpu.VMEM((len(rows), tokens, width), dtype),
+            pltpu.VMEM((slots, width), dtype),
+            pltpu.SemaphoreType.DMA((len(rows), pieces)),
+            pltpu.SemaphoreType.DMA((pieces,)),
+        ],
         cost_estimate=pl.CostEstimate(
             flops=2 * tokens * slots * width,
             bytes_accessed=2 * width * (tokens + slots),
@@ -398,7 +426,7 @@
             slot_ref[d, 0] = sums
 
 
-def product(table, entry, rows, weight, saved, gates, copies, earlier=()):
+def product(table, entry, rows, weight, saved, gates, copies, grant, earlier=()):
     slots, width = rows.shape
     hidden = weight.shape[0]
     total = saved.shape[0]
@@ -427,7 +455,7 @@
             scratch_shapes=[pltpu.VMEM((slots, LANES), jnp.float32)],
         ),
         input_output_aliases={5 + i: i for i in range(len(earlier))},
-        compiler_params=pltpu.CompilerParams(vmem_limit_bytes=PRODUCT_VMEM),
+        compiler_params=pltpu.CompilerParams(vmem_limit_bytes=grant),
         cost_estimate=pl.CostEstimate(
             flops=2 * slots * width * hidden,
             bytes_accessed=2 * (slots * width + hidden * width + 2 * slots * hidden),
@@ -591,8 +619,8 @@
     own_rows = send(mine, [cotangent])
     other_rows = send(other, swapped)
     *saved, gates, own = forward(everyone, cube, groups, top_count, capacity, targets)
-    result = product(table, 0, own_rows, weight, hidden, gates, experts)
-    result = product(table, 1, other_rows, weight, hidden, gates, experts, result)
+    result = product(table, 0, own_rows, weight, hidden, gates, experts, OWN_VMEM)
+    result = product(table, 1, other_rows, weight, hidden, gates, experts, OTHER_VMEM, result)
     hidden_grad, slot_grad = result
     slot_grads = lax.all_to_all(slot_grad, AXES, split_axis=0, concat_axis=0)
     d_group, d_expert = adjoint(slot_grads, saved, own, groups, capacity, targets)

time: 156 us -> 159 us (1.019)
  local copies, waits for them, and re-layouts: 3.2 us -> 10.3 us
  Pallas kernels: 37.2 us -> 34 us
    unnamed x31 -> x37, local copies, waits for them, and re-layouts: 3.16 us -> 8.79 us
    pallas_call x2, Pallas kernels: 13.7 us -> 10.9 us  [product(): pl.pallas_call(product_kernel, out_shape=[jax.ShapeDtypeStruct((total, hi...]
  transfers between devices with their start and end apart: 10 -> 10, of which waited for: 5 -> 4; matrix products, arithmetic and copies ran while one was open for 0% -> 3% of each run, Pallas kernels for 13% -> 11%
where the time goes in v5:
time: 159 us; the launch traced here: 158 us
  waiting for transfers between devices  75.3 us (47%)
  Pallas kernels  34 us (21%)
  starting transfers between devices  27.7 us (17%)
  local copies, waits for them, and re-layouts  10.3 us (6%)
  blocking collectives  10.2 us (6%)
    ppermute x3, waiting for transfers between devices, replicated(): column.append(lax.ppermute(mine, AXES, pairs))  61.7 us
    ppermute x3, waiting for transfers between devices, replicated(): everyone = jnp.concatenate([everyone, lax.ppermute(everyone, AXES, pairs)])  13.5 us
    pallas_call x2, Pallas kernels, product(): pl.pallas_call(product_kernel, out_shape=[jax.ShapeDtypeStruct((total, hi...  10.9 us
    all_to_all x2, starting transfers between devices, send(): got = lax.all_to_all(packed, NEAR, split_axis=0, concat_axis=0)  10.8 us
    all_to_all x1, blocking collectives, replicated(): slot_grads = lax.all_to_all(slot_grad, AXES, split_axis=0, concat_axis=0)  10.2 us
    pallas_call x1, Pallas kernels, forward(): pl.pallas_call(partial(forward_kernel, groups=groups, top_count=top_count...  9.87 us
    unnamed x37, local copies, waits for them, and re-layouts  8.79 us
    pallas_call x2, Pallas kernels, pack_rows(): pl.pallas_call(partial(pack_kernel, near=near, capacity=capacity, first_i...  8.18 us
  transfers between devices with their start and end apart: 10, of which 4 were waited for; matrix products, arithmetic and copies ran while one was open for 3% of the time, Pallas kernels for 11%

profile of v5, /device:TPU:0, one launch (start us, length us, event | category | flops | bytes accessed | tf_op | source)
XLA Modules:
  0.0 158.3 jit_solution(7150363517302028459)
XLA Ops:
  0.6 1.4 mine.1.small_ref
  2.0 4.0 %pack_rows.3 = bf16[256,3584]{1,0:T(8,128)(2,1)} custom-call(f32[40,128]{1,0:T(8,128)} %mine.1.small_ref, bf16[128,3584]{1,0:T(8,128)(2,1)} %refs_0_.1), custom_call_target="tpu_custom_call" | custom-call | flops 234881024 | bytes 2752512 | tf_op jit(solution)/shard_map/pack_rows/pallas_call | solution.py:210
  6.0 0.0 copy-start.13
  6.0 6.3 %all-to-all-start.1 = ((bf16[16,16,3584]{2,1,0:T(8,128)(2,1)}), bf16[16,16,3584]{2,1,0:T(8,128)(2,1)S(1)}, u32[]{:S(2)}, u32[]{:S(2)}) async-start(bf16[16,16,3584]{2,1,0:T(8,128)(2,1)} %bitcast.36), calls=%async_computation.1 | async-start | bytes 3670016 | tf_op jit(solution)/shard_map/all_to_all | solution.py:615
  12.4 4.6 %collective-permute-start.1 = (bf16[128,3584]{1,0:T(8,128)(2,1)}, bf16[128,3584]{1,0:T(8,128)(2,1)S(1)}, u32[]{:S(2)}, u32[]{:S(2)}) collective-permute-start(bf16[128,3584]{1,0:T(8,128)(2,1)} %refs_0_.1), channel_id=1, source_target_pairs={{0,16},{24,8},{1,17},{25,9},{2,18},{26,10},{3,19},{27,11},{4,20},{... | collective-permute-start | bytes 2752520 | tf_op jit(solution)/shard_map/ppermute | solution.py:610
  16.9 1.3 collective-permute-start.2
  18.2 0.0 copy-done.13
  18.2 4.5 %collective-permute-start = (f32[40,128]{1,0:T(8,128)S(1)}, f32[40,128]{1,0:T(8,128)S(1)}, u32[]{:S(2)}, u32[]{:S(2)}) collective-permute-start(f32[40,128]{1,0:T(8,128)S(1)} %copy-done.13), channel_id=1, source_target_pairs={{0,16},{1,17},{2,18},{3,19},{4,20},{5,21},{6,22},{7,23},{8,24},{9,... | collective-permute-start | bytes 61448 | tf_op jit(solution)/shard_map/ppermute | solution.py:599
  22.7 40.2 %collective-permute-done.small_ref = f32[40,128]{1,0:T(8,128)S(1)} collective-permute-done((f32[40,128]{1,0:T(8,128)S(1)}, f32[40,128]{1,0:T(8,128)S(1)}, u32[]{:S(2)}, u32[]{:S(2)}) %collective-permute-start) | collective-permute-done | bytes 20512 | tf_op jit(solution)/shard_map/ppermute | solution.py:599
  62.9 0.0 copy-start.14
  62.9 0.0 collective-permute-done.1.refs_0_
  62.9 0.0 copy-start.12
  62.9 0.0 collective-permute-done.2.refs_1_
  62.9 0.6 copy-done.14
  63.5 0.3 copy-done.12
  63.8 4.2 %pack_rows.2 = bf16[256,3584]{1,0:T(8,128)(2,1)} custom-call(f32[40,128]{1,0:T(8,128)} %copy-done.14, bf16[128,3584]{1,0:T(8,128)(2,1)} %copy-done.12, bf16[128,3584]{1,0:T(8,128)(2,1)} %collective-permute-done.2.refs_1_), custom_call_target="tpu_custom_call" | custom-call | flops 234881024 | bytes 2752512 | tf_op jit(solution)/shard_map/pack_rows/pallas_call | solution.py:210
  68.0 0.0 all-to-all-done.1
  68.0 0.0 copy-start.15
  68.0 4.4 %all-to-all-start = ((bf16[16,16,3584]{2,1,0:T(8,128)(2,1)}), bf16[16,16,3584]{2,1,0:T(8,128)(2,1)}, u32[]{:S(2)}, u32[]{:S(2)}) async-start(bf16[16,16,3584]{2,1,0:T(8,128)(2,1)} %bitcast.35), calls=%async_computation | async-start | bytes 3670016 | tf_op jit(solution)/shard_map/all_to_all | solution.py:615
  72.5 0.0 copy-start.1
  72.5 2.2 %collective-permute-start.4 = (f32[40,128]{1,0:T(8,128)S(1)}, f32[40,128]{1,0:T(8,128)S(1)}, u32[]{:S(2)}, u32[]{:S(2)}) collective-permute-start(f32[40,128]{1,0:T(8,128)S(1)} %copy-done.13), channel_id=1, source_target_pairs={{0,24},{1,25},{2,26},{3,27},{4,28},{5,29},{6,30},{7,31},{8,16},{9,... | collective-permute-start | bytes 61448 | tf_op jit(solution)/shard_map/ppermute | solution.py:599
  74.6 0.0 collective-permute-start.3
  74.6 0.6 constant_dynamic-update-slice_fusion.10
  75.3 21.5 %collective-permute-done.4 = f32[40,128]{1,0:T(8,128)S(1)} collective-permute-done((f32[40,128]{1,0:T(8,128)S(1)}, f32[40,128]{1,0:T(8,128)S(1)}, u32[]{:S(2)}, u32[]{:S(2)}) %collective-permute-start.4) | collective-permute-done | bytes 20512 | tf_op jit(solution)/shard_map/ppermute | solution.py:599
  96.8 0.0 collective-permute-done.3
  96.8 0.0 copy-done.15
  96.8 0.1 collective-permute-start.5
  96.9 0.6 constant_dynamic-update-slice_fusion.9
  97.5 0.6 constant_dynamic-update-slice_fusion.8
  98.1 0.6 constant_dynamic-update-slice_fusion.7
  98.7 0.0 collective-permute-done.5
  98.7 0.7 constant_dynamic-update-slice_fusion.6
  99.4 3.4 %collective-permute-start.6 = (f32[8,40,128]{2,1,0:T(8,128)S(1)}, f32[8,40,128]{2,1,0:T(8,128)S(1)}, u32[]{:S(2)}, u32[]{:S(2)}) collective-permute-start(f32[8,40,128]{2,1,0:T(8,128)S(1)} %get-tuple-element.35), channel_id=1, source_target_pairs={{0,2},{1,3},{2,0},{3,1},{4,6},{5,7},{6,4},{7,5},{8,10},{9,11},{10,... | collective-permute-start | bytes 491528 | tf_op jit(solution)/shard_map/ppermute | solution.py:605
  102.9 4.9 %collective-permute-done.6 = f32[8,40,128]{2,1,0:T(8,128)S(1)} collective-permute-done((f32[8,40,128]{2,1,0:T(8,128)S(1)}, f32[8,40,128]{2,1,0:T(8,128)S(1)}, u32[]{:S(2)}, u32[]{:S(2)}) %collective-permute-start.6) | collective-permute-done | bytes 163872 | tf_op jit(solution)/shard_map/ppermute | solution.py:605
  107.7 0.7 constant_dynamic-update-slice_fusion.5
  108.4 1.0 collective-permute-start.7
  109.4 0.1 pad_add_fusion.table_ref
  109.5 0.0 copy-start.11
  109.5 8.7 %collective-permute-done.7 = f32[16,40,128]{2,1,0:T(8,128)S(1)} collective-permute-done((f32[16,40,128]{2,1,0:T(8,128)}, f32[16,40,128]{2,1,0:T(8,128)S(1)}, u32[]{:S(2)}, u32[]{:S(2)}) %collective-permute-start.7) | collective-permute-done | bytes 327712 | tf_op jit(solution)/shard_map/ppermute | solution.py:605
  118.2 0.7 constant_dynamic-update-slice_fusion.11.all_ref
  118.9 9.9 %forward.1 = (f32[6,32,40,128]{3,2,1,0:T(8,128)}, f32[5,32,8,128]{3,2,1,0:T(8,128)}, f32[5,40,128]{2,1,0:T(8,128)}, f32[32,32,128]{2,1,0:T(8,128)}, f32[32,32,12...) custom-call(f32[32,40,128]{2,1,0:T(8,128)} %constant_dynamic-update-slice_fusion.11.all_ref), custom_call_target="tpu_custom_call" | custom-call | flops 10000000 | bytes 8000000 | tf_op jit(solution)/shard_map/forward/pallas_call | solution.py:378
  128.8 0.0 copy-done.1
  128.8 0.0 copy-start
  128.8 3.1 %copy-done = bf16[1,1024,3584]{2,1,0:T(8,128)(2,1)S(1)} copy-done((bf16[1,1024,3584]{2,1,0:T(8,128)(2,1)S(1)}, bf16[1,1024,3584]{2,1,0:T(8,128)(2,1)}, u32[]{:S(2)}) %copy-start) | copy-done | bytes 7340056
  131.9 0.0 copy-start.3
  131.9 0.9 copy-done.3
  132.8 3.8 %product.2 = (bf16[512,1024]{1,0:T(8,128)(2,1)}, f32[32,2,1,256]{3,2,1,0:T(1,128)S(1)}) custom-call(s32[2]{0:T(128)S(1)} %pad_add_fusion.table_ref, bf16[256,3584]{1,0:T(8,128)(2,1)S(1)} %bitcast.32, bf16[1024,3584]{1,0:T(8,128)(2,1)S(1)} %bitcast.31, bf16[512,1024]{1,0:T(8,128)(2,1)S(1)} %bitcast.34, f32[512,128]{1,0:T(8,128)S(1)} %copy-done.3), custom_call_target="tpu_custom_call" | custom-call | flops 1879048192 | bytes 10223616 | tf_op jit(solution)/shard_map/product/pallas_call | solution.py:435
  136.6 0.0 copy-done.11
  136.6 0.6 copy-done.8
  137.3 0.0 all-to-all-done
  137.3 0.0 copy-start.6
  137.3 0.0 copy-start.7
  137.3 0.0 copy-start.9
  137.3 0.0 copy-start.10
  137.3 7.1 %product.3 = (bf16[512,1024]{1,0:T(8,128)(2,1)}, f32[32,2,1,256]{3,2,1,0:T(1,128)}) custom-call(s32[2]{0:T(128)} %copy-done.11, bf16[256,3584]{1,0:T(8,128)(2,1)} %bitcast.6.rows_ref, bf16[1024,3584]{1,0:T(8,128)(2,1)} %bitcast.30, bf16[512,1024]{1,0:T(8,128)(2,1)} %bitcast.33, ...), custom_call_target="tpu_custom_call", output_to_operand_aliasing={{0}: (5, {}), {1}: (6, {})} | custom-call | flops 1879048192 | bytes 10223616 | tf_op jit(solution)/shard_map/product/pallas_call | solution.py:435
  144.4 10.2 %all_to_all.15.answer_ref = f32[32,2,1,256]{3,2,1,0:T(1,128)S(1)} all-to-all(f32[32,2,1,256]{3,2,1,0:T(1,128)} %get-tuple-element.21), channel_id=1, replica_groups=mesh['half'=2,'plane'=2,'expert'=8] {'half','plane','expert'}, dimensions={0} | all-to-all | bytes 131072 | tf_op jit(solution)/shard_map/all_to_all | solution.py:625
  154.6 0.0 copy-done.2
  154.6 0.0 copy-done.4
  154.6 0.0 copy-done.5
  154.6 0.0 copy-done.6
  154.7 0.0 copy-done.7
  154.7 0.0 copy-done.9
  154.7 0.0 copy-done.10
  154.7 3.6 %adjoint.1 = (f32[4,128]{1,0:T(4,128)}, f32[32,128]{1,0:T(8,128)}) custom-call(f32[32,2,1,256]{3,2,1,0:T(1,128)S(1)} %all_to_all.15.answer_ref, f32[6,32,40,128]{3,2,1,0:T(8,128)S(1)} %copy-done.2, f32[5,32,8,128]{3,2,1,0:T(8,128)S(1)} %copy-done.4, f32[5,40,128]{2,1,0:T(8,128)S(1)} %copy-done.9, f32[32,32,128]{2,1,0:T(8,128)S(1)} %copy-done.5, ...), custom_call_target="tpu_custom_call" | custom-call | flops 10000000 | bytes 8000000 | tf_op jit(solution)/shard_map/adjoint/pallas_call | solution.py:554
  (5 shorter events, 0.0 us)
Async XLA Ops:
  6.0 12.2 %copy-start.13 = (f32[40,128]{1,0:T(8,128)S(1)}, f32[40,128]{1,0:T(8,128)}, u32[]{:S(2)}) copy-start(f32[40,128]{1,0:T(8,128)} %mine.1.small_ref) | copy-start | bytes 61444
  6.0 62.0 %all-to-all-start.1 = ((bf16[16,16,3584]{2,1,0:T(8,128)(2,1)}), bf16[16,16,3584]{2,1,0:T(8,128)(2,1)S(1)}, u32[]{:S(2)}, u32[]{:S(2)}) async-start(bf16[16,16,3584]{2,1,0:T(8,128)(2,1)} %bitcast.36), calls=%async_computation.1 | async-start | bytes 3670016 | tf_op jit(solution)/shard_map/all_to_all | solution.py:615
  12.4 50.5 %collective-permute-start.1 = (bf16[128,3584]{1,0:T(8,128)(2,1)}, bf16[128,3584]{1,0:T(8,128)(2,1)S(1)}, u32[]{:S(2)}, u32[]{:S(2)}) collective-permute-start(bf16[128,3584]{1,0:T(8,128)(2,1)} %refs_0_.1), channel_id=1, source_target_pairs={{0,16},{24,8},{1,17},{25,9},{2,18},{26,10},{3,19},{27,11},{4,20},{... | collective-permute-start | bytes 2752520 | tf_op jit(solution)/shard_map/ppermute | solution.py:610
  16.9 46.0 %collective-permute-start.2 = (bf16[128,3584]{1,0:T(8,128)(2,1)}, bf16[128,3584]{1,0:T(8,128)(2,1)}, u32[]{:S(2)}, u32[]{:S(2)}) collective-permute-start(bf16[128,3584]{1,0:T(8,128)(2,1)} %refs_0_.1), channel_id=1, source_target_pairs={{8,24},{16,0},{9,25},{17,1},{10,26},{18,2},{11,27},{19,3},{12,28},... | collective-permute-start | bytes 2752520 | tf_op jit(solution)/shard_map/ppermute | solution.py:610
  18.2 44.7 %collective-permute-start = (f32[40,128]{1,0:T(8,128)S(1)}, f32[40,128]{1,0:T(8,128)S(1)}, u32[]{:S(2)}, u32[]{:S(2)}) collective-permute-start(f32[40,128]{1,0:T(8,128)S(1)} %copy-done.13), channel_id=1, source_target_pairs={{0,16},{1,17},{2,18},{3,19},{4,20},{5,21},{6,22},{7,23},{8,24},{9,... | collective-permute-start | bytes 61448 | tf_op jit(solution)/shard_map/ppermute | solution.py:599
  62.9 0.6 copy-start.14
  62.9 0.9 copy-start.12
  68.0 28.8 %copy-start.15 = (f32[40,128]{1,0:T(8,128)S(1)}, f32[40,128]{1,0:T(8,128)}, u32[]{:S(2)}) copy-start(f32[40,128]{1,0:T(8,128)} %copy-done.14) | copy-start | bytes 61444
  68.0 69.2 %all-to-all-start = ((bf16[16,16,3584]{2,1,0:T(8,128)(2,1)}), bf16[16,16,3584]{2,1,0:T(8,128)(2,1)}, u32[]{:S(2)}, u32[]{:S(2)}) async-start(bf16[16,16,3584]{2,1,0:T(8,128)(2,1)} %bitcast.35), calls=%async_computation | async-start | bytes 3670016 | tf_op jit(solution)/shard_map/all_to_all | solution.py:615
  72.5 56.3 %copy-start.1 = (bf16[1,512,1024]{2,1,0:T(8,128)(2,1)S(1)}, bf16[1,512,1024]{2,1,0:T(8,128)(2,1)}, u32[]{:S(2)}) copy-start(bf16[1,512,1024]{2,1,0:T(8,128)(2,1)} %param.10) | copy-start | bytes 3145732
  72.5 24.3 %collective-permute-start.4 = (f32[40,128]{1,0:T(8,128)S(1)}, f32[40,128]{1,0:T(8,128)S(1)}, u32[]{:S(2)}, u32[]{:S(2)}) collective-permute-start(f32[40,128]{1,0:T(8,128)S(1)} %copy-done.13), channel_id=1, source_target_pairs={{0,24},{1,25},{2,26},{3,27},{4,28},{5,29},{6,30},{7,31},{8,16},{9,... | collective-permute-start | bytes 61448 | tf_op jit(solution)/shard_map/ppermute | solution.py:599
  74.6 22.2 %collective-permute-start.3 = (f32[40,128]{1,0:T(8,128)S(1)}, f32[40,128]{1,0:T(8,128)S(1)}, u32[]{:S(2)}, u32[]{:S(2)}) collective-permute-start(f32[40,128]{1,0:T(8,128)S(1)} %copy-done.13), channel_id=1, source_target_pairs={{0,8},{1,9},{2,10},{3,11},{4,12},{5,13},{6,14},{7,15},{8,0},{9,1},... | collective-permute-start | bytes 61448 | tf_op jit(solution)/shard_map/ppermute | solution.py:599
  96.8 1.9 %collective-permute-start.5 = (f32[4,40,128]{2,1,0:T(8,128)S(1)}, f32[4,40,128]{2,1,0:T(8,128)S(1)}, u32[]{:S(2)}, u32[]{:S(2)}) collective-permute-start(f32[4,40,128]{2,1,0:T(8,128)S(1)} %pad_maximum_fusion), channel_id=1, source_target_pairs={{0,1},{1,0},{2,3},{3,2},{4,5},{5,4},{6,7},{7,6},{8,9},{9,8},{10,11... | collective-permute-start | bytes 245768 | tf_op jit(solution)/shard_map/ppermute | solution.py:605
  99.4 8.3 %collective-permute-start.6 = (f32[8,40,128]{2,1,0:T(8,128)S(1)}, f32[8,40,128]{2,1,0:T(8,128)S(1)}, u32[]{:S(2)}, u32[]{:S(2)}) collective-permute-start(f32[8,40,128]{2,1,0:T(8,128)S(1)} %get-tuple-element.35), channel_id=1, source_target_pairs={{0,2},{1,3},{2,0},{3,1},{4,6},{5,7},{6,4},{7,5},{8,10},{9,11},{10,... | collective-permute-start | bytes 491528 | tf_op jit(solution)/shard_map/ppermute | solution.py:605
  108.4 9.7 %collective-permute-start.7 = (f32[16,40,128]{2,1,0:T(8,128)}, f32[16,40,128]{2,1,0:T(8,128)S(1)}, u32[]{:S(2)}, u32[]{:S(2)}) collective-permute-start(f32[16,40,128]{2,1,0:T(8,128)} %get-tuple-element.31), channel_id=1, source_target_pairs={{0,4},{1,5},{2,6},{3,7},{4,0},{5,1},{6,2},{7,3},{8,12},{9,13},{10,... | collective-permute-start | bytes 983048 | tf_op jit(solution)/shard_map/ppermute | solution.py:605
  109.5 27.1 %copy-start.11 = (s32[2]{0:T(128)}, s32[2]{0:T(128)S(1)}, u32[]{:S(2)}) copy-start(s32[2]{0:T(128)S(1)} %pad_add_fusion.table_ref) | copy-start | bytes 28
  128.8 3.1 %copy-start = (bf16[1,1024,3584]{2,1,0:T(8,128)(2,1)S(1)}, bf16[1,1024,3584]{2,1,0:T(8,128)(2,1)}, u32[]{:S(2)}) copy-start(bf16[1,1024,3584]{2,1,0:T(8,128)(2,1)} %param.11) | copy-start | bytes 22020100
  131.9 0.9 copy-start.3
  136.6 0.6 copy-start.8
  137.3 17.4 %copy-start.2 = (f32[6,32,40,128]{3,2,1,0:T(8,128)S(1)}, f32[6,32,40,128]{3,2,1,0:T(8,128)}, u32[]{:S(2)}) copy-start(f32[6,32,40,128]{3,2,1,0:T(8,128)} %get-tuple-element.22.level_ref) | copy-start | bytes 11796484
  137.3 17.4 %copy-start.4 = (f32[5,32,8,128]{3,2,1,0:T(8,128)S(1)}, f32[5,32,8,128]{3,2,1,0:T(8,128)}, u32[]{:S(2)}) copy-start(f32[5,32,8,128]{3,2,1,0:T(8,128)} %get-tuple-element.23.inverse_ref) | copy-start | bytes 1966084
  137.3 17.4 %copy-start.5 = (f32[32,32,128]{2,1,0:T(8,128)S(1)}, f32[32,32,128]{2,1,0:T(8,128)}, u32[]{:S(2)}) copy-start(f32[32,32,128]{2,1,0:T(8,128)} %get-tuple-element.25.seed_q_ref) | copy-start | bytes 1572868
  137.3 17.4 %copy-start.6 = (f32[32,32,128]{2,1,0:T(8,128)S(1)}, f32[32,32,128]{2,1,0:T(8,128)}, u32[]{:S(2)}) copy-start(f32[32,32,128]{2,1,0:T(8,128)} %get-tuple-element.26.seed_p_ref) | copy-start | bytes 1572868
  137.3 17.4 %copy-start.7 = (s32[32,32,128]{2,1,0:T(8,128)S(1)}, s32[32,32,128]{2,1,0:T(8,128)}, u32[]{:S(2)}) copy-start(s32[32,32,128]{2,1,0:T(8,128)} %get-tuple-element.27.where_ref) | copy-start | bytes 1572868
  137.3 17.4 %copy-start.9 = (f32[5,40,128]{2,1,0:T(8,128)S(1)}, f32[5,40,128]{2,1,0:T(8,128)}, u32[]{:S(2)}) copy-start(f32[5,40,128]{2,1,0:T(8,128)} %get-tuple-element.24.column_ref) | copy-start | bytes 307204
  137.3 17.4 %copy-start.10 = (f32[40,128]{1,0:T(8,128)S(1)}, f32[40,128]{1,0:T(8,128)}, u32[]{:S(2)}) copy-start(f32[40,128]{1,0:T(8,128)} %get-tuple-element.28.own_ref) | copy-start | bytes 61444
